TPU v7x, 32 devices: a whole 2x2x4 slice. The times are simulated.
32 devices in a mesh: dp: 4 (over y, x), expert: 8 (over z, core).
Axes of the slice: x: 2, y: 2, z: 4, core: 2. Of those that a mesh axis runs over, the one named last changes fastest.
Arguments:
- tokens: bfloat16 [1024, 2048], P(('dp', 'expert')), may hold values from -6 to 6
- grad_out: bfloat16 [1024, 2048], P(('dp', 'expert')), may hold values from -0.59765625 to 0.59765625
- routing: int32 [1024, 8], P(('dp', 'expert')), may hold values from 0 to 15, as said below
- replica: int32 [1024, 8], P(('dp', 'expert')), may hold values from 0 to 1, as said below
- gates: bfloat16 [1024, 8], P(('dp', 'expert')), may hold values from 0.25 to 4
- host_expert: int32 [8], replicated, may hold values from 0 to 15, as said below
- w_gate_up: bfloat16 [16, 2, 768, 2048], P('expert', None, 'dp'), may hold values from -0.125 to 0.125
- w_down: bfloat16 [16, 768, 2048], P('expert', 'dp'), may hold values from -0.21875 to 0.21875
Outputs:
- grad_tokens: bfloat16 [1024, 2048], P(('dp', 'expert'))
- grad_gates: float32 [1024, 8], P(('dp', 'expert'))
- grad_w_gate_up: bfloat16 [16, 2, 768, 2048], P('expert', None, 'dp')
- grad_w_down: bfloat16 [16, 768, 2048], P('expert', 'dp')
Inputs may be any that keep to these rules, and one draw needn't show every extreme that they name: `routing`: column k of a token names an expert of 2 * k to 2 * k + 1. Within the rows of one device, experts 2 i and 2 i + 1 are named together exactly 2 * 16 times. `replica`: within the rows of one device, each expert has at most 16 choices marked 0 and at most 16 marked 1; some expert reaches 16 marked 0 from every device, and in every index of dp some expert reaches 16 marked 1 from every device. Only experts listed in host_expert have choices marked 1. `host_expert`: for every device d of the expert axis exactly one of its experts 2 d and 2 d + 1 is listed, and it is listed once.
All inputs are finite; a program needn't handle non-finite values.
Results may differ from a plain program's by a relative error of at most 0.013.
Values may be sent and summed in bfloat16 or wider, within the bound.
A program may use at most 128 MiB of HBM per device.

v0:
```python
import functools

import jax
import jax.numpy as jnp
from jax import lax
from jax.experimental import pallas as pl
from jax.experimental.pallas import tpu as pltpu
from jax.sharding import PartitionSpec as P

MESH = pl.DeviceIdType.MESH


def lookup(values_table, indices):
    matches = indices[..., None] == lax.broadcasted_iota(
        jnp.int32, indices.shape + values_table.shape, indices.ndim
    )
    return jnp.sum(jnp.where(matches, values_table, 0), axis=-1)


def placement(host_expert, owned_experts, devices):
    experts = owned_experts * devices
    matches = host_expert[None, :] == lax.broadcasted_iota(jnp.int32, (experts, devices), 0)
    helper_ids = lax.broadcasted_iota(jnp.int32, (experts, devices), 1)
    helper_of = jnp.sum(jnp.where(matches, helper_ids, 0), axis=1)
    listed = jnp.sum(matches.astype(jnp.int32), axis=1)
    return (helper_of, listed)


def targets(routing, replica, host_expert, owned_experts, devices, slot_rows, groups):
    helper_of, listed = placement(host_expert, owned_experts, devices)
    choices = routing.shape[0] // groups * routing.shape[1]
    usable = (replica == 0) | (lookup(listed, routing) > 0)
    device_to = jnp.where(replica == 0, routing // owned_experts, lookup(helper_of, routing))
    block_to = jnp.where(replica == 0, routing % owned_experts, owned_experts)
    labels = (routing * 2 + replica).reshape(groups, choices)
    earlier = lax.broadcasted_iota(jnp.int32, (choices, choices), 1) < lax.broadcasted_iota(
        jnp.int32, (choices, choices), 0
    )
    matching = (labels[:, :, None] == labels[:, None, :]) & earlier[None]
    ranking = jnp.sum(matching.astype(jnp.int32), axis=2).reshape(routing.shape)
    group_ids = lax.broadcasted_iota(jnp.int32, (groups, choices), 0).reshape(routing.shape)
    position = ((block_to * groups + group_ids) * devices + device_to) * slot_rows + ranking
    return jnp.where(usable, position, -1)


def selector(position, total_slots):
    matches = position[None, :, :] == lax.broadcasted_iota(
        jnp.int32, (total_slots,) + position.shape, 0
    )
    picker = jnp.sum(matches.astype(jnp.float32), axis=2).astype(jnp.bfloat16)
    return (matches, picker)


def fill_rows(matches, picker, tokens, grad_out, gates):
    row_x = jnp.dot(picker, tokens, preferred_element_type=jnp.float32).astype(jnp.bfloat16)
    row_dy = jnp.dot(picker, grad_out, preferred_element_type=jnp.float32).astype(jnp.bfloat16)
    row_gate = jnp.sum(
        jnp.where(matches, gates[None].astype(jnp.float32), 0.0), axis=(1, 2)
    ).astype(jnp.bfloat16)
    return (row_x, row_dy, row_gate)


def expert_block(inputs, upstream, weight, gate_up, down_matrix):
    mixed = jnp.einsum("rd,jfd->jrf", inputs, gate_up, preferred_element_type=jnp.float32)
    gate_pre = mixed[0]
    up_part = mixed[1]
    sigmoid_gate = jax.nn.sigmoid(gate_pre)
    active = gate_pre * sigmoid_gate
    hidden = (active * up_part).astype(jnp.bfloat16)
    output_part = jnp.einsum("rf,fd->rd", hidden, down_matrix, preferred_element_type=jnp.float32)
    gate_part = jnp.sum(output_part * upstream.astype(jnp.float32), axis=1)
    scaled = (weight.astype(jnp.float32)[:, None] * upstream.astype(jnp.float32)).astype(
        jnp.bfloat16
    )
    grad_hidden = jnp.einsum("rd,fd->rf", scaled, down_matrix, preferred_element_type=jnp.float32)
    grad_gate = grad_hidden * up_part * sigmoid_gate * (1.0 + gate_pre * (1.0 - sigmoid_gate))
    grad_mixed = jnp.stack([grad_gate, grad_hidden * active], axis=0).astype(jnp.bfloat16)
    input_part = jnp.einsum("jrf,jfd->rd", grad_mixed, gate_up, preferred_element_type=jnp.float32)
    weight_gu = jnp.einsum("jrf,rd->jfd", grad_mixed, inputs, preferred_element_type=jnp.float32)
    weight_down = jnp.einsum("rf,rd->fd", hidden, scaled, preferred_element_type=jnp.float32)
    return (input_part, gate_part, weight_gu, weight_down)


def shards(tokens, grad_out, routing, replica, gates, host_expert, w_gate_up, w_down):
    devices = lax.axis_size("expert")
    device_id = lax.axis_index("expert")
    token_rows, features = tokens.shape
    owned_experts = w_gate_up.shape[0]
    quarter = w_down.shape[1]
    topk_width = routing.shape[1]
    slot_rows = token_rows * topk_width // (owned_experts * devices)
    blocks = owned_experts + 1
    lane_rows = devices * slot_rows
    piece_rows = quarter // devices
    home_slots = targets(routing, replica, host_expert, owned_experts, devices, slot_rows, 1)
    home_matches, home_picker = selector(home_slots, blocks * lane_rows)
    row_x, row_dy, row_gate = fill_rows(home_matches, home_picker, tokens, grad_out, gates)
    sent_x, sent_dy, sent_gate = (
        lax.all_to_all(
            row_x.reshape(blocks, lane_rows, features),
            "expert",
            split_axis=1,
            concat_axis=1,
            tiled=True,
        ),
        lax.all_to_all(
            row_dy.reshape(blocks, lane_rows, features),
            "expert",
            split_axis=1,
            concat_axis=1,
            tiled=True,
        ),
        lax.all_to_all(
            row_gate.reshape(blocks, lane_rows), "expert", split_axis=1, concat_axis=1, tiled=True
        ),
    )
    block_x, block_dy, block_gate = (
        lax.all_gather(sent_x, "dp", axis=1, tiled=True),
        lax.all_gather(sent_dy, "dp", axis=1, tiled=True),
        lax.all_gather(sent_gate, "dp", axis=1, tiled=True),
    )
    owner_of_helper = host_expert // owned_experts
    owns_copy = owner_of_helper == device_id
    copied_local = jnp.sum(jnp.where(owns_copy, host_expert % owned_experts, 0))
    helper_ids = lax.broadcasted_iota(jnp.int32, (devices, devices), 1)
    owner_ids = lax.broadcasted_iota(jnp.int32, (devices, devices), 0)
    helper_of_owner = jnp.sum(
        jnp.where(owner_of_helper[None, :] == owner_ids, helper_ids, 0), axis=1
    )
    source_gu = lax.dynamic_index_in_dim(w_gate_up, copied_local, 0, keepdims=False)
    source_down = lax.dynamic_index_in_dim(w_down, copied_local, 0, keepdims=False)
    spread_gu, spread_down = (
        lax.all_to_all(
            source_gu.reshape(2, devices, piece_rows, features),
            "expert",
            split_axis=1,
            concat_axis=1,
            tiled=True,
        ),
        lax.all_to_all(
            source_down.reshape(1, devices, piece_rows, features),
            "expert",
            split_axis=1,
            concat_axis=1,
            tiled=True,
        ),
    )
    spread_gu = jnp.take(spread_gu, owner_of_helper, axis=1)
    spread_down = jnp.take(spread_down, owner_of_helper, axis=1)
    hosted_gu, hosted_down = (
        lax.all_to_all(spread_gu, "expert", split_axis=1, concat_axis=1, tiled=True),
        lax.all_to_all(spread_down, "expert", split_axis=1, concat_axis=1, tiled=True),
    )
    hosted_gu = hosted_gu.reshape(2, quarter, features)
    hosted_down = hosted_down.reshape(quarter, features)
    input_parts = []
    gate_parts = []
    owner_gu = []
    owner_down = []
    for block in range(blocks):
        if block < owned_experts:
            gate_up = w_gate_up[block]
            down_matrix = w_down[block]
        else:
            gate_up = hosted_gu
            down_matrix = hosted_down
        input_part, gate_part, weight_gu, weight_down = expert_block(
            block_x[block], block_dy[block], block_gate[block], gate_up, down_matrix
        )
        input_parts.append(input_part.astype(jnp.bfloat16))
        gate_parts.append(gate_part.astype(jnp.bfloat16))
        owner_gu.append(weight_gu)
        owner_down.append(weight_down)
    helper_gu = owner_gu[owned_experts].astype(jnp.bfloat16)
    helper_down = owner_down[owned_experts].astype(jnp.bfloat16)
    back_gu, back_down = (
        lax.all_to_all(
            helper_gu.reshape(2, devices, piece_rows, features),
            "expert",
            split_axis=1,
            concat_axis=1,
            tiled=True,
        ),
        lax.all_to_all(
            helper_down.reshape(1, devices, piece_rows, features),
            "expert",
            split_axis=1,
            concat_axis=1,
            tiled=True,
        ),
    )
    back_gu = jnp.take(back_gu, helper_of_owner, axis=1)
    back_down = jnp.take(back_down, helper_of_owner, axis=1)
    extra_gu, extra_down = (
        lax.all_to_all(back_gu, "expert", split_axis=1, concat_axis=1, tiled=True),
        lax.all_to_all(back_down, "expert", split_axis=1, concat_axis=1, tiled=True),
    )
    extra_gu = extra_gu.reshape(2, quarter, features).astype(jnp.float32)
    extra_down = extra_down.reshape(quarter, features).astype(jnp.float32)
    stacked_dx = jnp.stack(input_parts, axis=0)
    stacked_dg = jnp.stack(gate_parts, axis=0)
    summed_dx, summed_dg = (
        lax.psum_scatter(stacked_dx, "dp", scatter_dimension=1, tiled=True).astype(jnp.float32),
        lax.psum_scatter(stacked_dg, "dp", scatter_dimension=1, tiled=True).astype(jnp.float32),
    )
    row_dx = summed_dx.astype(jnp.bfloat16)
    row_dg = summed_dg.astype(jnp.bfloat16)
    home_dx, home_dg = (
        lax.all_to_all(row_dx, "expert", split_axis=1, concat_axis=1, tiled=True),
        lax.all_to_all(row_dg, "expert", split_axis=1, concat_axis=1, tiled=True),
    )
    home_dx = home_dx.reshape(blocks * lane_rows, features)
    home_dg = home_dg.reshape(blocks * lane_rows).astype(jnp.float32)
    grad_tokens = jnp.einsum(
        "st,sd->td", home_picker, home_dx, preferred_element_type=jnp.float32
    ).astype(jnp.bfloat16)
    grad_gates = jnp.sum(jnp.where(home_matches, home_dg[:, None, None], 0.0), axis=0)
    grad_gu = []
    grad_down = []
    for block in range(owned_experts):
        present = (copied_local == block).astype(jnp.float32)
        grad_gu.append((owner_gu[block] + present * extra_gu).astype(jnp.bfloat16))
        grad_down.append((owner_down[block] + present * extra_down).astype(jnp.bfloat16))
    return (grad_tokens, grad_gates, jnp.stack(grad_gu, axis=0), jnp.stack(grad_down, axis=0))


def chosen_gates(routing, replica, gates, host_expert, experts):
    listed = jnp.any(routing[:, :, None] == host_expert[None, None, :], axis=2)
    usable = (replica == 0) | listed
    picks = usable[:, :, None] & (
        routing[:, :, None] == lax.broadcasted_iota(jnp.int32, routing.shape + (experts,), 2)
    )
    weights = jnp.sum(jnp.where(picks, gates.astype(jnp.float32)[:, :, None], 0.0), axis=1)
    return (picks, weights)


def greet(partners):
    barrier = pltpu.get_barrier_semaphore()
    for condition, device in partners:

        @pl.when(condition)
        def _():
            pl.semaphore_signal(barrier, inc=1, device_id=device, device_id_type=MESH)

    pl.semaphore_wait(barrier, sum(condition.astype(jnp.int32) for condition, _ in partners))


def fused_kernel(
    depth,
    features,
    source,
    gu_hbm,
    down_hbm,
    summed_ref,
    grad_gu_hbm,
    grad_down_hbm,
    rows_ref,
    gu_ref,
    down_ref,
    grad_gu_ref,
    grad_down_ref,
    mixed_ref,
    hidden_ref,
    part_ref,
    paired,
    ready,
    crossed,
    column_ref,
    risen,
    total,
    sent,
    landed,
    local,
    sums_sent,
    sums_landed,
):
    dp = lax.axis_index("dp")
    expert = lax.axis_index("expert")
    height, core = expert // 2, expert % 2
    row, column = dp // 2, dp % 2
    across = row * 2 + 1 - column
    along = (1 - row) * 2 + column
    diagonal = (1 - row) * 2 + 1 - column
    roles = (dp, across, along, diagonal)
    count, half = source.shape[0], source.shape[0] // 2
    owned = down_ref.shape[0]
    group_slots = 2 * depth
    group_rows = group_slots * count
    lanes = source.shape[1] - 2 * features
    partner = (dp, height * 2 + 1 - core)
    x_device = (across, expert)
    y_device = (along, expert)
    up_device = (dp, jnp.minimum(expert + 2, 2 * depth - 1))
    down_device = (dp, jnp.maximum(expert - 2, 0))
    has_up = height < depth - 1
    has_down = height > 0
    always = height >= 0
    levels = [lax.rem(height + step, depth) for step in range(1, depth)] + [height]
    loads = [
        pltpu.make_async_copy(gu_hbm, gu_ref, local.at[1]),
        pltpu.make_async_copy(down_hbm, down_ref, local.at[2]),
    ]
    for load in loads:
        load.start()
    greet(
        [
            (always, partner),
            (always, x_device),
            (always, y_device),
            (always, (diagonal, expert)),
        ]
        + [(always, (dp, level * 2 + core)) for level in levels[:-1]]
    )

    def slot_of(dp_from, height_from, core_from):
        return (dp_from * depth + height_from) * 2 + core_from

    def copy(slot, way, device, part=None, own=False):
        block = source if own else rows_ref.at[slot]
        into = rows_ref.at[slot]
        piece = 0
        if part is not None:
            block = block.at[pl.ds(part * half, half)]
            into = into.at[pl.ds(part * half, half)]
            piece = part
        return pltpu.make_async_remote_copy(
            src_ref=block,
            dst_ref=into,
            send_sem=sent.at[slot, way * 2 + piece],
            recv_sem=landed.at[slot, piece],
            device_id=device,
            device_id_type=MESH,
        )

    finish = []

    def guard(condition, action):
        if condition is always:
            action()
        else:
            pl.when(condition)(action)

    def send(condition, *args, **kwargs):
        finish.append((condition, args, kwargs))
        guard(condition, lambda: copy(*args, **kwargs).start())

    def arrive(condition, slot, part=None):
        guard(condition, lambda: copy(slot, 0, partner, part).wait_recv())

    def both(first, second):
        return first if second is always else jnp.logical_and(first, second)

    steps = [[(always, height)]]
    for distance in range(1, depth):
        steps.append([(height >= distance, jnp.maximum(height - distance, 0))])
        steps[-1].append(
            (height + distance < depth, jnp.minimum(height + distance, depth - 1))
        )

    def relay_column(index):
        for side, (condition, level) in enumerate(steps[index]):
            slot = slot_of(dp, level, core)
            arrive(condition, slot)
            if side == 0:
                send(both(condition, has_up), slot, 3, up_device)
            else:
                send(both(condition, has_down), slot, 4, down_device)
            send(condition, slot, 1, x_device)
            send(condition, slot, 2, y_device)
            send(condition, slot, 0, partner)

    def relay_sides(index):
        for condition, level in steps[index]:
            slot = slot_of(across, level, core)
            arrive(condition, slot)
            send(condition, slot, 2, y_device, part=0)
            send(condition, slot, 0, partner)
            slot = slot_of(along, level, core)
            arrive(condition, slot)
            send(condition, slot, 1, x_device, part=1)
            send(condition, slot, 0, partner)

    def relay_diagonal(index):
        for condition, level in steps[index]:
            slot = slot_of(diagonal, level, core)
            for part in range(2):
                arrive(condition, slot, part)
                send(condition, slot, 0, partner, part=part)

    def partner_rows(role):
        for level in range(depth):
            slot = slot_of(roles[role], level, 1 - core)
            if role == 3:
                arrive(always, slot, 0)
                arrive(always, slot, 1)
            else:
                arrive(always, slot)

    def remote(block, into, index, device):
        return pltpu.make_async_remote_copy(
            src_ref=block,
            dst_ref=into,
            send_sem=sums_sent.at[index],
            recv_sem=sums_landed.at[index],
            device_id=device,
            device_id_type=MESH,
        )

    def pair_copy(role):
        return remote(part_ref.at[roles[role], :, 1 - core], paired.at[role], role, partner)

    def cross_copy(step, way):
        return remote(
            ready.at[step, way],
            crossed.at[step, way],
            4 + step * 3 + way,
            (roles[way + 1], expert),
        )

    def rise_copy(step):
        return remote(
            column_ref.at[step],
            risen.at[step],
            4 + 3 * depth + step,
            (dp, levels[step] * 2 + core),
        )

    def group(role):
        return pl.ds(roles[role] * group_slots, group_slots)

    def rows_by_columns(a, b):
        return lax.dot_general(
            a, b, (((1,), (1,)), ((), ())), preferred_element_type=jnp.float32
        )

    def compute(role):
        inputs = rows_ref[group(role), :, :features].reshape(group_rows, features)
        upstream = rows_ref[group(role), :, features : 2 * features].reshape(
            group_rows, features
        )
        side = rows_ref[group(role), :, 2 * features :].reshape(group_rows, lanes)
        side = side.astype(jnp.float32)
        slots = lax.broadcasted_iota(jnp.int32, side.shape, 1)
        gate_side = jnp.zeros(side.shape, jnp.float32)
        for local_expert in range(owned):
            at_expert = slots == expert * owned + local_expert
            weight = jnp.sum(jnp.where(at_expert, side, 0.0), axis=1, keepdims=True)
            gate_pre = rows_by_columns(inputs, gu_ref[local_expert, 0])
            up_part = rows_by_columns(inputs, gu_ref[local_expert, 1])
            raw_hidden = rows_by_columns(upstream, down_ref[local_expert])
            sigmoid_gate = jax.nn.sigmoid(gate_pre)
            active = gate_pre * sigmoid_gate
            hidden = (active * up_part).astype(jnp.bfloat16).astype(jnp.float32)
            gate_part = jnp.sum(hidden * raw_hidden, axis=1, keepdims=True)
            gate_side = jnp.where(at_expert, gate_part, gate_side)
            grad_hidden = raw_hidden * weight
            grad_gate = (
                grad_hidden * up_part * sigmoid_gate * (1.0 + gate_pre * (1.0 - sigmoid_gate))
            )
            hidden_ref[local_expert, roles[role]] = (hidden * weight).astype(jnp.bfloat16)
            mixed_ref[2 * local_expert, roles[role]] = grad_gate.astype(jnp.bfloat16)
            mixed_ref[2 * local_expert + 1, roles[role]] = (grad_hidden * active).astype(
                jnp.bfloat16
            )
        dx = jnp.zeros((group_rows, features), jnp.float32)
        for index in range(2 * owned):
            dx = dx + jnp.dot(
                mixed_ref[index, roles[role]],
                gu_ref[index // 2, index % 2],
                preferred_element_type=jnp.float32,
            )
        shape = (depth, 2, count)
        part_ref[roles[role], :, :, :, :features] = dx.astype(jnp.bfloat16).reshape(
            shape + (features,)
        )
        part_ref[roles[role], :, :, :, features:] = gate_side.astype(jnp.bfloat16).reshape(
            shape + (lanes,)
        )
        pair_copy(role).start()

    def combine(role):
        pair_copy(role).wait_recv()
        if role > 0:
            for step in range(depth):
                ready[step, role - 1] = (
                    part_ref[roles[role], levels[step], core].astype(jnp.float32)
                    + paired[role, levels[step]].astype(jnp.float32)
                ).astype(jnp.bfloat16)
                cross_copy(step, role - 1).start()

    def columns_by_columns(a, b):
        return lax.dot_general(
            a, b, (((0,), (0,)), ((), ())), preferred_element_type=jnp.float32
        ).astype(jnp.bfloat16)

    total_rows = 4 * group_rows
    quarter = mixed_ref.shape[3]

    def down_grads():
        upstream = rows_ref[:, :, features : 2 * features].reshape(total_rows, features)
        for local_expert in range(owned):
            weighted = hidden_ref[local_expert].reshape(total_rows, quarter)
            grad_down_ref[local_expert] = columns_by_columns(weighted, upstream)
        pltpu.make_async_copy(grad_down_ref, grad_down_hbm, local.at[2]).start()

    def gu_grads():
        inputs = rows_ref[:, :, :features].reshape(total_rows, features)
        for index in range(2 * owned):
            grads = mixed_ref[index].reshape(total_rows, quarter)
            grad_gu_ref[index // 2, index % 2] = columns_by_columns(grads, inputs)
        pltpu.make_async_copy(grad_gu_ref, grad_gu_hbm, local.at[1]).start()

    mine = slot_of(dp, height, core)
    send(has_up, mine, 3, up_device, own=True)
    send(has_down, mine, 4, down_device, own=True)
    send(always, mine, 1, x_device, own=True)
    send(always, mine, 2, y_device, own=True)
    send(always, mine, 0, partner, own=True)
    keep = pltpu.make_async_copy(source, rows_ref.at[mine], local.at[0])
    keep.start()
    for index in range(1, depth):
        relay_column(index)
        relay_sides(index - 1)
    keep.wait()
    for load in loads:
        load.wait()
    partner_rows(0)
    compute(0)
    relay_sides(depth - 1)
    relay_diagonal(0)
    partner_rows(1)
    compute(1)
    for index in range(1, depth - 1):
        relay_diagonal(index)
    partner_rows(2)
    compute(2)
    combine(0)
    combine(1)
    relay_diagonal(depth - 1)
    partner_rows(3)
    compute(3)
    combine(2)
    down_grads()
    combine(3)
    gu_grads()
    for step in range(depth):
        for way in range(3):
            cross_copy(step, way).wait_recv()
        summed = part_ref[dp, levels[step], core].astype(jnp.float32) + paired[
            0, levels[step]
        ].astype(jnp.float32)
        for way in range(3):
            summed = summed + crossed[step, way].astype(jnp.float32)
        if step < depth - 1:
            column_ref[step] = summed.astype(jnp.bfloat16)
            rise_copy(step).start()
        else:
            total[...] = summed
    for step in range(depth - 1):
        rise_copy(step).wait_recv()
        total[...] = total[...] + risen[step].astype(jnp.float32)
    summed_ref[...] = total[...].astype(jnp.bfloat16)
    for condition, args, kwargs in finish:
        guard(condition, lambda args=args, kwargs=kwargs: copy(*args, **kwargs).wait_send())
    for role in range(4):
        pair_copy(role).wait_send()
    for step in range(depth):
        for way in range(3):
            cross_copy(step, way).wait_send()
        if step < depth - 1:
            rise_copy(step).wait_send()
    pltpu.make_async_copy(grad_down_ref, grad_down_hbm, local.at[2]).wait()
    pltpu.make_async_copy(grad_gu_ref, grad_gu_hbm, local.at[1]).wait()


def fused_layer(payload, w_gate_up, w_down, expert_size):
    count, width = payload.shape
    features = w_down.shape[2]
    owned, quarter = w_down.shape[:2]
    depth = expert_size // 2
    slots = 4 * expert_size
    sums = width - features
    block = (count, sums)
    group_rows = expert_size * count
    kind = jnp.bfloat16
    anywhere = pl.BlockSpec(memory_space=pl.ANY)
    return pl.pallas_call(
        functools.partial(fused_kernel, depth, features),
        out_shape=(
            jax.ShapeDtypeStruct(block, kind),
            jax.ShapeDtypeStruct(w_gate_up.shape, kind),
            jax.ShapeDtypeStruct(w_down.shape, kind),
        ),
        in_specs=[anywhere] * 3,
        out_specs=(pl.BlockSpec(memory_space=pltpu.VMEM), anywhere, anywhere),
        scratch_shapes=[
            pltpu.VMEM((slots, count, width), kind),
            pltpu.VMEM(w_gate_up.shape, kind),
            pltpu.VMEM(w_down.shape, kind),
            pltpu.VMEM(w_gate_up.shape, kind),
            pltpu.VMEM(w_down.shape, kind),
            pltpu.VMEM((2 * owned, 4, group_rows, quarter), kind),
            pltpu.VMEM((owned, 4, group_rows, quarter), kind),
            pltpu.VMEM((4, depth, 2) + block, kind),
            pltpu.VMEM((4, depth) + block, kind),
            pltpu.VMEM((depth, 3) + block, kind),
            pltpu.VMEM((depth, 3) + block, kind),
            pltpu.VMEM((depth,) + block, kind),
            pltpu.VMEM((depth,) + block, kind),
            pltpu.VMEM(block, jnp.float32),
            pltpu.SemaphoreType.DMA((slots, 10)),
            pltpu.SemaphoreType.DMA((slots, 2)),
            pltpu.SemaphoreType.DMA((3,)),
            pltpu.SemaphoreType.DMA((4 + 4 * depth,)),
            pltpu.SemaphoreType.DMA((4 + 4 * depth,)),
        ],
        compiler_params=pltpu.CompilerParams(
            collective_id=0, has_side_effects=True, vmem_limit_bytes=60 << 20
        ),
    )(payload, w_gate_up, w_down)


def gathered_shards(
    tokens, grad_out, routing, replica, gates, host_expert, w_gate_up, w_down
):
    devices = lax.axis_size("expert")
    features = tokens.shape[1]
    owned = w_gate_up.shape[0]
    experts = owned * devices
    lanes = (experts + 127) // 128 * 128
    picks, weights = chosen_gates(routing, replica, gates, host_expert, experts)
    side = jnp.pad(weights.astype(jnp.bfloat16), ((0, 0), (0, lanes - experts)))
    payload = jnp.concatenate([tokens, grad_out, side], axis=1)
    summed, grad_gu, grad_down = fused_layer(payload, w_gate_up, w_down, devices)
    grad_tokens = summed[:, :features]
    sums = summed[:, features : features + experts].astype(jnp.float32)
    grad_gates = jnp.sum(jnp.where(picks, sums[:, None, :], 0.0), axis=2)
    return (grad_tokens, grad_gates, grad_gu, grad_down)


def serve(tokens, grad_out, routing, replica, gates, host_expert, w_gate_up, w_down):
    squares = lax.axis_size("dp") == 4 and lax.axis_size("expert") % 2 == 0
    visits_all = routing.shape[1] >= lax.axis_size("expert")
    body = gathered_shards if squares and visits_all else shards
    return body(tokens, grad_out, routing, replica, gates, host_expert, w_gate_up, w_down)


def solution(mesh):
    in_specs = (
        P(("dp", "expert"), None),
        P(("dp", "expert"), None),
        P(("dp", "expert"), None),
        P(("dp", "expert"), None),
        P(("dp", "expert"), None),
        P(),
        P("expert", None, "dp", None),
        P("expert", "dp", None),
    )
    out_specs = (
        P(("dp", "expert"), None),
        P(("dp", "expert"), None),
        P("expert", None, "dp", None),
        P("expert", "dp", None),
    )
    return jax.shard_map(serve, mesh=mesh, in_specs=in_specs, out_specs=out_specs, check_vma=False)
```

profile of v0, /device:TPU:0, one launch (start us, length us, event | category | flops | bytes accessed | tf_op | source)
XLA Modules:
  0.0 95.3 jit_solution(8590913730055413207)
XLA Ops:
  0.6 0.0 copy-start.1
  0.6 0.8 compare_reduce_fusion
  1.5 0.7 compare_or_fusion
  2.2 0.7 convert_element_type.11
  2.9 0.7 select_reduce_fusion.1
  3.6 0.1 copy.18
  3.7 1.7 %fusion.1.source = bf16[32,4224]{1,0:T(8,128)(2,1)} fusion(bf16[32,16]{1,0:T(8,128)(2,1)S(1)} %copy.18, bf16[32,2048]{1,0:T(8,128)(2,1)} %param.9, bf16[32,2048]{1,0:T(8,128)(2,1)} %param.8), kind=kLoop, calls=%fused_computation.2 | loop fusion | flops 1081344 | bytes 533504 | tf_op jit(solution)/shard_map/concatenate | solution.py:633
  5.4 81.7 %shard_map.111 = (bf16[32,2176]{1,0:T(8,128)(2,1)}, bf16[2,2,192,2048]{3,2,1,0:T(8,128)(2,1)}, bf16[2,192,2048]{2,1,0:T(8,128)(2,1)}) custom-call(bf16[32,4224]{1,0:T(8,128)(2,1)} %fusion.1.source, bf16[2,2,192,2048]{3,2,1,0:T(8,128)(2,1)} %gu_hbm.1, bf16[2,192,2048]{2,1,0:T(8,128)(2,1)} %down_hbm.1), custom_call_target="tpu_custom_call" | custom-call | tf_op jit(solution)/shard_map/pallas_call | solution.py:587
  87.1 0.7 slice_convert_fusion
  87.8 0.1 copy.19
  87.9 0.0 copy-done.1
  87.9 0.6 select_reduce_fusion
  88.5 1.6 %slice.6 = bf16[32,2048]{1,0:T(8,128)(2,1)} slice(bf16[32,2176]{1,0:T(8,128)(2,1)} %get-tuple-element.7), slice={[0:32], [0:2048]} | slice | bytes 262144 | tf_op jit(solution)/shard_map/slice | solution.py:635
  90.1 0.0 copy-start
  90.1 4.1 %copy.22 = bf16[2,2,192,2048]{3,2,1,0:T(8,128)(2,1)} copy(bf16[2,2,192,2048]{3,2,1,0:T(8,128)(2,1)} %get-tuple-element.16) | data formatting | bytes 6291456
  94.2 0.0 copy-done
  94.2 1.1 %copy.23 = bf16[2,192,2048]{2,1,0:T(8,128)(2,1)} copy(bf16[2,192,2048]{2,1,0:T(8,128)(2,1)S(1)} %copy-done) | data formatting | bytes 3145728
Async XLA Ops:
  0.6 87.3 %copy-start.1 = (s32[32,8]{0,1:T(8,128)S(1)}, s32[32,8]{0,1:T(8,128)}, u32[]{:S(2)}) copy-start(s32[32,8]{0,1:T(8,128)} %param.10) | copy-start | bytes 3076
  90.1 4.1 %copy-start = (bf16[2,192,2048]{2,1,0:T(8,128)(2,1)S(1)}, bf16[2,192,2048]{2,1,0:T(8,128)(2,1)}, u32[]{:S(2)}) copy-start(bf16[2,192,2048]{2,1,0:T(8,128)(2,1)} %get-tuple-element.17) | copy-start | bytes 4718596
where the time goes:
time: 95.6 us; the launch traced here: 95.3 us
  Pallas kernels  81.7 us (85%)
  local copies, waits for them, and re-layouts  6.97 us (7%)
  other arithmetic  5.95 us (6%)
    pallas_call x1, Pallas kernels, fused_layer(): pl.pallas_call(functools.partial(fused_kernel, depth, features), out_shap...  81.7 us
    unnamed x6, local copies, waits for them, and re-layouts  5.24 us

commit v1 on v0

v1 whole, which is shorter than its diff:
```python
import functools

import jax
import jax.numpy as jnp
from jax import lax
from jax.experimental import pallas as pl
from jax.experimental.pallas import tpu as pltpu
from jax.sharding import PartitionSpec as P

MESH = pl.DeviceIdType.MESH


def lookup(values_table, indices):
    matches = indices[..., None] == lax.broadcasted_iota(
        jnp.int32, indices.shape + values_table.shape, indices.ndim
    )
    return jnp.sum(jnp.where(matches, values_table, 0), axis=-1)


def placement(host_expert, owned_experts, devices):
    experts = owned_experts * devices
    matches = host_expert[None, :] == lax.broadcasted_iota(jnp.int32, (experts, devices), 0)
    helper_ids = lax.broadcasted_iota(jnp.int32, (experts, devices), 1)
    helper_of = jnp.sum(jnp.where(matches, helper_ids, 0), axis=1)
    listed = jnp.sum(matches.astype(jnp.int32), axis=1)
    return (helper_of, listed)


def targets(routing, replica, host_expert, owned_experts, devices, slot_rows, groups):
    helper_of, listed = placement(host_expert, owned_experts, devices)
    choices = routing.shape[0] // groups * routing.shape[1]
    usable = (replica == 0) | (lookup(listed, routing) > 0)
    device_to = jnp.where(replica == 0, routing // owned_experts, lookup(helper_of, routing))
    block_to = jnp.where(replica == 0, routing % owned_experts, owned_experts)
    labels = (routing * 2 + replica).reshape(groups, choices)
    earlier = lax.broadcasted_iota(jnp.int32, (choices, choices), 1) < lax.broadcasted_iota(
        jnp.int32, (choices, choices), 0
    )
    matching = (labels[:, :, None] == labels[:, None, :]) & earlier[None]
    ranking = jnp.sum(matching.astype(jnp.int32), axis=2).reshape(routing.shape)
    group_ids = lax.broadcasted_iota(jnp.int32, (groups, choices), 0).reshape(routing.shape)
    position = ((block_to * groups + group_ids) * devices + device_to) * slot_rows + ranking
    return jnp.where(usable, position, -1)


def selector(position, total_slots):
    matches = position[None, :, :] == lax.broadcasted_iota(
        jnp.int32, (total_slots,) + position.shape, 0
    )
    picker = jnp.sum(matches.astype(jnp.float32), axis=2).astype(jnp.bfloat16)
    return (matches, picker)


def fill_rows(matches, picker, tokens, grad_out, gates):
    row_x = jnp.dot(picker, tokens, preferred_element_type=jnp.float32).astype(jnp.bfloat16)
    row_dy = jnp.dot(picker, grad_out, preferred_element_type=jnp.float32).astype(jnp.bfloat16)
    row_gate = jnp.sum(
        jnp.where(matches, gates[None].astype(jnp.float32), 0.0), axis=(1, 2)
    ).astype(jnp.bfloat16)
    return (row_x, row_dy, row_gate)


def expert_block(inputs, upstream, weight, gate_up, down_matrix):
    mixed = jnp.einsum("rd,jfd->jrf", inputs, gate_up, preferred_element_type=jnp.float32)
    gate_pre = mixed[0]
    up_part = mixed[1]
    sigmoid_gate = jax.nn.sigmoid(gate_pre)
    active = gate_pre * sigmoid_gate
    hidden = (active * up_part).astype(jnp.bfloat16)
    output_part = jnp.einsum("rf,fd->rd", hidden, down_matrix, preferred_element_type=jnp.float32)
    gate_part = jnp.sum(output_part * upstream.astype(jnp.float32), axis=1)
    scaled = (weight.astype(jnp.float32)[:, None] * upstream.astype(jnp.float32)).astype(
        jnp.bfloat16
    )
    grad_hidden = jnp.einsum("rd,fd->rf", scaled, down_matrix, preferred_element_type=jnp.float32)
    grad_gate = grad_hidden * up_part * sigmoid_gate * (1.0 + gate_pre * (1.0 - sigmoid_gate))
    grad_mixed = jnp.stack([grad_gate, grad_hidden * active], axis=0).astype(jnp.bfloat16)
    input_part = jnp.einsum("jrf,jfd->rd", grad_mixed, gate_up, preferred_element_type=jnp.float32)
    weight_gu = jnp.einsum("jrf,rd->jfd", grad_mixed, inputs, preferred_element_type=jnp.float32)
    weight_down = jnp.einsum("rf,rd->fd", hidden, scaled, preferred_element_type=jnp.float32)
    return (input_part, gate_part, weight_gu, weight_down)


def shards(tokens, grad_out, routing, replica, gates, host_expert, w_gate_up, w_down):
    devices = lax.axis_size("expert")
    device_id = lax.axis_index("expert")
    token_rows, features = tokens.shape
    owned_experts = w_gate_up.shape[0]
    quarter = w_down.shape[1]
    topk_width = routing.shape[1]
    slot_rows = token_rows * topk_width // (owned_experts * devices)
    blocks = owned_experts + 1
    lane_rows = devices * slot_rows
    piece_rows = quarter // devices
    home_slots = targets(routing, replica, host_expert, owned_experts, devices, slot_rows, 1)
    home_matches, home_picker = selector(home_slots, blocks * lane_rows)
    row_x, row_dy, row_gate = fill_rows(home_matches, home_picker, tokens, grad_out, gates)
    sent_x, sent_dy, sent_gate = (
        lax.all_to_all(
            row_x.reshape(blocks, lane_rows, features),
            "expert",
            split_axis=1,
            concat_axis=1,
            tiled=True,
        ),
        lax.all_to_all(
            row_dy.reshape(blocks, lane_rows, features),
            "expert",
            split_axis=1,
            concat_axis=1,
            tiled=True,
        ),
        lax.all_to_all(
            row_gate.reshape(blocks, lane_rows), "expert", split_axis=1, concat_axis=1, tiled=True
        ),
    )
    block_x, block_dy, block_gate = (
        lax.all_gather(sent_x, "dp", axis=1, tiled=True),
        lax.all_gather(sent_dy, "dp", axis=1, tiled=True),
        lax.all_gather(sent_gate, "dp", axis=1, tiled=True),
    )
    owner_of_helper = host_expert // owned_experts
    owns_copy = owner_of_helper == device_id
    copied_local = jnp.sum(jnp.where(owns_copy, host_expert % owned_experts, 0))
    helper_ids = lax.broadcasted_iota(jnp.int32, (devices, devices), 1)
    owner_ids = lax.broadcasted_iota(jnp.int32, (devices, devices), 0)
    helper_of_owner = jnp.sum(
        jnp.where(owner_of_helper[None, :] == owner_ids, helper_ids, 0), axis=1
    )
    source_gu = lax.dynamic_index_in_dim(w_gate_up, copied_local, 0, keepdims=False)
    source_down = lax.dynamic_index_in_dim(w_down, copied_local, 0, keepdims=False)
    spread_gu, spread_down = (
        lax.all_to_all(
            source_gu.reshape(2, devices, piece_rows, features),
            "expert",
            split_axis=1,
            concat_axis=1,
            tiled=True,
        ),
        lax.all_to_all(
            source_down.reshape(1, devices, piece_rows, features),
            "expert",
            split_axis=1,
            concat_axis=1,
            tiled=True,
        ),
    )
    spread_gu = jnp.take(spread_gu, owner_of_helper, axis=1)
    spread_down = jnp.take(spread_down, owner_of_helper, axis=1)
    hosted_gu, hosted_down = (
        lax.all_to_all(spread_gu, "expert", split_axis=1, concat_axis=1, tiled=True),
        lax.all_to_all(spread_down, "expert", split_axis=1, concat_axis=1, tiled=True),
    )
    hosted_gu = hosted_gu.reshape(2, quarter, features)
    hosted_down = hosted_down.reshape(quarter, features)
    input_parts = []
    gate_parts = []
    owner_gu = []
    owner_down = []
    for block in range(blocks):
        if block < owned_experts:
            gate_up = w_gate_up[block]
            down_matrix = w_down[block]
        else:
            gate_up = hosted_gu
            down_matrix = hosted_down
        input_part, gate_part, weight_gu, weight_down = expert_block(
            block_x[block], block_dy[block], block_gate[block], gate_up, down_matrix
        )
        input_parts.append(input_part.astype(jnp.bfloat16))
        gate_parts.append(gate_part.astype(jnp.bfloat16))
        owner_gu.append(weight_gu)
        owner_down.append(weight_down)
    helper_gu = owner_gu[owned_experts].astype(jnp.bfloat16)
    helper_down = owner_down[owned_experts].astype(jnp.bfloat16)
    back_gu, back_down = (
        lax.all_to_all(
            helper_gu.reshape(2, devices, piece_rows, features),
            "expert",
            split_axis=1,
            concat_axis=1,
            tiled=True,
        ),
        lax.all_to_all(
            helper_down.reshape(1, devices, piece_rows, features),
            "expert",
            split_axis=1,
            concat_axis=1,
            tiled=True,
        ),
    )
    back_gu = jnp.take(back_gu, helper_of_owner, axis=1)
    back_down = jnp.take(back_down, helper_of_owner, axis=1)
    extra_gu, extra_down = (
        lax.all_to_all(back_gu, "expert", split_axis=1, concat_axis=1, tiled=True),
        lax.all_to_all(back_down, "expert", split_axis=1, concat_axis=1, tiled=True),
    )
    extra_gu = extra_gu.reshape(2, quarter, features).astype(jnp.float32)
    extra_down = extra_down.reshape(quarter, features).astype(jnp.float32)
    stacked_dx = jnp.stack(input_parts, axis=0)
    stacked_dg = jnp.stack(gate_parts, axis=0)
    summed_dx, summed_dg = (
        lax.psum_scatter(stacked_dx, "dp", scatter_dimension=1, tiled=True).astype(jnp.float32),
        lax.psum_scatter(stacked_dg, "dp", scatter_dimension=1, tiled=True).astype(jnp.float32),
    )
    row_dx = summed_dx.astype(jnp.bfloat16)
    row_dg = summed_dg.astype(jnp.bfloat16)
    home_dx, home_dg = (
        lax.all_to_all(row_dx, "expert", split_axis=1, concat_axis=1, tiled=True),
        lax.all_to_all(row_dg, "expert", split_axis=1, concat_axis=1, tiled=True),
    )
    home_dx = home_dx.reshape(blocks * lane_rows, features)
    home_dg = home_dg.reshape(blocks * lane_rows).astype(jnp.float32)
    grad_tokens = jnp.einsum(
        "st,sd->td", home_picker, home_dx, preferred_element_type=jnp.float32
    ).astype(jnp.bfloat16)
    grad_gates = jnp.sum(jnp.where(home_matches, home_dg[:, None, None], 0.0), axis=0)
    grad_gu = []
    grad_down = []
    for block in range(owned_experts):
        present = (copied_local == block).astype(jnp.float32)
        grad_gu.append((owner_gu[block] + present * extra_gu).astype(jnp.bfloat16))
        grad_down.append((owner_down[block] + present * extra_down).astype(jnp.bfloat16))
    return (grad_tokens, grad_gates, jnp.stack(grad_gu, axis=0), jnp.stack(grad_down, axis=0))


OWN, ACROSS, ALONG, DIAGONAL = range(4)
PARTNER, TO_X, TO_Y, INNER, OUTER = range(5)
OWN_X, OWN_Y, OWN_INNER, OWN_OUTER, ACROSS_Y, ALONG_X, DIAGONAL_INNER, DIAGONAL_OUTER = range(8)
ALL, END, MID = range(3)


def usable_choices(routing, replica, host_ref):
    usable = replica == 0
    for index in range(host_ref.shape[0]):
        usable = usable | (routing == host_ref[index])
    return usable


def fused_kernel(
    experts,
    tokens_hbm,
    grad_out_hbm,
    routing_hbm,
    replica_hbm,
    gates_hbm,
    host_hbm,
    gu_hbm,
    down_hbm,
    tokens_out,
    gates_out,
    grad_gu_ref,
    grad_down_ref,
    rows_ref,
    gu_ref,
    down_ref,
    mixed_ref,
    hidden_ref,
    part_ref,
    paired_ref,
    inbox_ref,
    routing_ref,
    replica_ref,
    gates_ref,
    host_ref,
    local,
    sent,
    landed,
    pair_sent,
    pair_landed,
    sums_sent,
    sums_landed,
):
    dp = lax.axis_index("dp")
    expert = lax.axis_index("expert")
    height, core = expert // 2, expert % 2
    row, column = dp // 2, dp % 2
    depth = rows_ref.shape[0] // 4
    count = rows_ref.shape[2]
    half = count // 2
    features = tokens_hbm.shape[1]
    lanes = rows_ref.shape[3] - 2 * features
    owned, quarter = down_ref.shape[:2]
    across = row * 2 + 1 - column
    along = (1 - row) * 2 + column
    roles = (dp, across, along, (1 - row) * 2 + 1 - column)
    upper = height // (depth // 2)
    levels = (
        height,
        height + 1 - 2 * (height % 2),
        depth // 2 - upper,
        (depth - 1) * (1 - upper),
    )
    is_mid = (height + upper) % 2 == 1
    is_end = (height + upper) % 2 == 0
    inner_level = height + 1 - 2 * upper
    targets_of = (
        (dp, height * 2 + 1 - core),
        (across, expert),
        (along, expert),
        (dp, inner_level * 2 + core),
        (dp, levels[1] * 2 + core),
    )
    scope = [ALL]
    unsent = ([], [], [])

    def within(role, body):
        scope[0] = role

        @pl.when(is_end if role == END else is_mid)
        def _():
            body()

        scope[0] = ALL

    def begin(make, *args):
        make(*args).start()
        unsent[scope[0]].append((make, args))

    def chip(role, near):
        return roles[role] * depth + levels[near]

    mine = chip(OWN, 0)
    loads = [
        pltpu.make_async_copy(routing_hbm, routing_ref, local.at[0]),
        pltpu.make_async_copy(replica_hbm, replica_ref, local.at[1]),
        pltpu.make_async_copy(gates_hbm, gates_ref, local.at[2]),
        pltpu.make_async_copy(host_hbm, host_ref, local.at[3]),
        pltpu.make_async_copy(tokens_hbm, rows_ref.at[mine, core, :, pl.ds(0, features)], local.at[4]),
        pltpu.make_async_copy(
            grad_out_hbm, rows_ref.at[mine, core, :, pl.ds(features, features)], local.at[5]
        ),
        pltpu.make_async_copy(gu_hbm, gu_ref, local.at[6]),
        pltpu.make_async_copy(down_hbm, down_ref, local.at[7]),
    ]
    for load in loads:
        load.start()
    barrier = pltpu.get_barrier_semaphore()
    for way in (PARTNER, TO_X, TO_Y, INNER):
        pl.semaphore_signal(barrier, inc=1, device_id=targets_of[way], device_id_type=MESH)

    @pl.when(is_mid)
    def _():
        pl.semaphore_signal(barrier, inc=1, device_id=targets_of[OUTER], device_id_type=MESH)

    for load in loads[:4]:
        load.wait()
    routing = routing_ref[...]
    usable = usable_choices(routing, replica_ref[...], host_ref)
    gates = jnp.where(usable, gates_ref[...].astype(jnp.float32), 0.0)
    weights = jnp.concatenate(
        [
            jnp.sum(jnp.where(routing == index, gates, 0.0), axis=0, keepdims=True)
            for index in range(experts)
        ]
        + [jnp.zeros((lanes - experts, count), jnp.float32)],
        axis=0,
    )
    rows_ref[mine, core, :, 2 * features :] = weights.T.astype(jnp.bfloat16)
    for load in loads[4:6]:
        load.wait()
    pl.semaphore_wait(barrier, 4 + is_mid.astype(jnp.int32))

    def piece(part):
        return pl.ds(part * half, half)

    def row_copy(role, near, part, way):
        at = chip(role, near)
        block = rows_ref.at[at, core] if part is None else rows_ref.at[at, core, piece(part)]
        index = 0 if part is None else part
        return pltpu.make_async_remote_copy(
            src_ref=block,
            dst_ref=block,
            send_sem=sent.at[at, way * 2 + index],
            recv_sem=landed.at[at, core, index],
            device_id=targets_of[way],
            device_id_type=MESH,
        )

    def forward(role, near, part, *ways):
        for way in ways:
            begin(row_copy, role, near, part, way)

    def arrive(role, near, part):
        row_copy(role, near, part, PARTNER).wait_recv()

    def relay(role, near, part, *ways):
        arrive(role, near, part)
        forward(role, near, part, *ways)
        if part == 1:
            forward(role, near, None, PARTNER)

    def partner_rows(role, near):
        at = chip(role, near)
        block = rows_ref.at[at, 1 - core]
        pltpu.make_async_remote_copy(
            src_ref=block,
            dst_ref=block,
            send_sem=sent.at[at, 0],
            recv_sem=landed.at[at, 1 - core, 0],
            device_id=targets_of[PARTNER],
            device_id_type=MESH,
        ).wait_recv()

    def rows_by_columns(a, b):
        return lax.dot_general(
            a, b, (((1,), (1,)), ((), ())), preferred_element_type=jnp.float32
        )

    def columns_by_columns(a, b):
        return lax.dot_general(
            a, b, (((0,), (0,)), ((), ())), preferred_element_type=jnp.float32
        ).astype(jnp.bfloat16)

    chip_rows = 2 * count

    def pair_copy(at):
        return pltpu.make_async_remote_copy(
            src_ref=part_ref.at[at, 1 - core],
            dst_ref=paired_ref.at[at],
            send_sem=pair_sent.at[at],
            recv_sem=pair_landed.at[at],
            device_id=targets_of[PARTNER],
            device_id_type=MESH,
        )

    def compute(*group):
        chips = [chip(role, near) for role, near in group]
        for role, near in group:
            partner_rows(role, near)

        def take(first, size):
            return jnp.concatenate(
                [
                    rows_ref[at, :, :, first : first + size].reshape(chip_rows, size)
                    for at in chips
                ],
                axis=0,
            )

        inputs = take(0, features)
        upstream = take(features, features)
        side = take(2 * features, lanes).astype(jnp.float32)
        slots = lax.broadcasted_iota(jnp.int32, side.shape, 1)
        gate_side = jnp.zeros(side.shape, jnp.float32)
        grads = []
        for local_expert in range(owned):
            at_expert = slots == expert * owned + local_expert
            weight = jnp.sum(jnp.where(at_expert, side, 0.0), axis=1, keepdims=True)
            gate_pre = rows_by_columns(inputs, gu_ref[local_expert, 0])
            up_part = rows_by_columns(inputs, gu_ref[local_expert, 1])
            raw_hidden = rows_by_columns(upstream, down_ref[local_expert])
            sigmoid_gate = jax.nn.sigmoid(gate_pre)
            active = gate_pre * sigmoid_gate
            hidden = (active * up_part).astype(jnp.bfloat16).astype(jnp.float32)
            gate_part = jnp.sum(hidden * raw_hidden, axis=1, keepdims=True)
            gate_side = jnp.where(at_expert, gate_part, gate_side)
            grad_hidden = raw_hidden * weight
            grad_gate = (
                grad_hidden * up_part * sigmoid_gate * (1.0 + gate_pre * (1.0 - sigmoid_gate))
            )
            weighted = (hidden * weight).astype(jnp.bfloat16)
            grads.append(grad_gate.astype(jnp.bfloat16))
            grads.append((grad_hidden * active).astype(jnp.bfloat16))
            for index, at in enumerate(chips):
                span = slice(index * chip_rows, (index + 1) * chip_rows)
                hidden_ref[local_expert, at] = weighted[span]
                mixed_ref[2 * local_expert, at] = grads[-2][span]
                mixed_ref[2 * local_expert + 1, at] = grads[-1][span]
        dx = jnp.zeros(inputs.shape, jnp.float32)
        for index in range(2 * owned):
            dx = dx + jnp.dot(
                grads[index],
                gu_ref[index // 2, index % 2],
                preferred_element_type=jnp.float32,
            )
        for index, at in enumerate(chips):
            span = slice(index * chip_rows, (index + 1) * chip_rows)
            part_ref[at, :, :, :features] = (
                dx[span].astype(jnp.bfloat16).reshape(2, count, features)
            )
            part_ref[at, :, :, features:] = (
                gate_side[span].astype(jnp.bfloat16).reshape(2, count, lanes)
            )
            begin(pair_copy, at)

    def combine(*group):
        for role, near in group:
            at = chip(role, near)
            pair_copy(at).wait_recv()
            part_ref[at, core] = (
                part_ref[at, core].astype(jnp.float32) + paired_ref[at].astype(jnp.float32)
            ).astype(jnp.bfloat16)

    def box_index(box, role, near, part):
        return (box * depth + levels[near]) * 2 + part

    def sum_copy(role, near, part, way, box):
        index = box_index(box, role, near, part)
        return pltpu.make_async_remote_copy(
            src_ref=part_ref.at[chip(role, near), core, piece(part)],
            dst_ref=inbox_ref.at[index],
            send_sem=sums_sent.at[index],
            recv_sem=sums_landed.at[index],
            device_id=targets_of[way],
            device_id_type=MESH,
        )

    def incoming(role, near, part, box):
        index = box_index(box, role, near, part)
        sum_copy(role, near, part, PARTNER, box).wait_recv()
        return inbox_ref[index].astype(jnp.float32)

    def send_sum(role, near, part, way):
        if way == TO_X:
            box = ALONG_X if role == DIAGONAL else OWN_X
        elif way == TO_Y:
            box = ACROSS_Y if role == DIAGONAL else OWN_Y
        else:
            outward = way == INNER and scope[0] == END
            box = (OWN_OUTER if outward else OWN_INNER) if role == OWN else (
                DIAGONAL_OUTER if outward else DIAGONAL_INNER
            )
        begin(sum_copy, role, near, part, way, box)

    def gather_sums(role, near, part, way, *boxes):
        at = chip(role, near)
        if boxes:
            value = part_ref[at, core, piece(part)].astype(jnp.float32)
            for box in boxes:
                value = value + incoming(role, near, part, box)
            part_ref[at, core, piece(part)] = value.astype(jnp.bfloat16)
        send_sum(role, near, part, way)

    total_rows = 4 * depth * chip_rows

    def down_grad(local_expert):
        upstream = rows_ref[:, :, :, features : 2 * features].reshape(total_rows, features)
        weighted = hidden_ref[local_expert].reshape(total_rows, quarter)
        grad_down_ref[local_expert] = columns_by_columns(weighted, upstream)

    def gu_grad(index):
        inputs = rows_ref[:, :, :, :features].reshape(total_rows, features)
        grads = mixed_ref[index].reshape(total_rows, quarter)
        grad_gu_ref[index // 2, index % 2] = columns_by_columns(grads, inputs)

    forward(OWN, 0, 0, INNER, TO_X, TO_Y)
    within(MID, lambda: forward(OWN, 0, 0, OUTER))
    forward(OWN, 0, 1, INNER, TO_X, TO_Y)
    within(MID, lambda: forward(OWN, 0, 1, OUTER))
    forward(OWN, 0, None, PARTNER)

    def end_first():
        relay(ACROSS, 0, 0, TO_Y)
        relay(OWN, 1, 0, TO_X, TO_Y)
        relay(ALONG, 0, 0)
        relay(ALONG, 0, 1, TO_X)
        relay(OWN, 1, 1, TO_X, TO_Y)
        relay(ACROSS, 0, 1)

    def mid_first():
        relay(OWN, 1, 0, INNER, TO_X)
        relay(OWN, 2, 0, OUTER)
        relay(ACROSS, 0, 0, TO_Y)
        forward(OWN, 1, 0, TO_Y)
        relay(ALONG, 0, 0)
        relay(OWN, 1, 1, INNER)
        relay(OWN, 2, 1, OUTER)
        relay(ALONG, 0, 1, TO_X)
        forward(OWN, 1, 1, TO_X, TO_Y)
        relay(ACROSS, 0, 1)
        forward(OWN, 2, 0, TO_X, TO_Y)
        forward(OWN, 2, 1, TO_X, TO_Y)

    within(END, end_first)
    within(MID, mid_first)
    for load in loads[6:]:
        load.wait()
    compute((OWN, 0), (OWN, 1))

    def end_second():
        relay(DIAGONAL, 0, 0, INNER)
        relay(OWN, 2, 0, TO_X, TO_Y)
        relay(DIAGONAL, 0, 1, INNER)
        relay(OWN, 2, 1, TO_X, TO_Y)

    def mid_second():
        relay(OWN, 3, 0, OUTER)
        relay(DIAGONAL, 0, 0, INNER)
        relay(OWN, 3, 1, OUTER)
        relay(DIAGONAL, 0, 1, INNER)
        forward(OWN, 3, 0, TO_X, TO_Y)
        forward(OWN, 3, 1, TO_X, TO_Y)

    within(END, end_second)
    within(MID, mid_second)
    compute((ACROSS, 0), (ALONG, 0))

    def end_third():
        relay(ACROSS, 1, 0)
        relay(ALONG, 1, 0)
        relay(OWN, 3, 0, TO_X, TO_Y)

    def mid_third():
        relay(ACROSS, 1, 0)
        relay(ALONG, 1, 0)
        relay(DIAGONAL, 1, 0, INNER)
        relay(DIAGONAL, 2, 0, OUTER)

    within(END, end_third)
    within(MID, mid_third)
    compute((DIAGONAL, 0), (OWN, 2))
    combine((OWN, 0), (OWN, 1))

    def end_fourth():
        relay(ACROSS, 1, 1)
        relay(ALONG, 1, 1)
        relay(OWN, 3, 1, TO_X, TO_Y)
        forward(ACROSS, 1, 0, TO_Y)
        forward(ALONG, 1, 1, TO_X)

    def mid_fourth():
        relay(DIAGONAL, 1, 1, INNER)
        relay(DIAGONAL, 2, 1, OUTER)
        relay(ACROSS, 1, 1)
        relay(ALONG, 1, 1)

    within(END, end_fourth)
    within(MID, mid_fourth)
    compute((ACROSS, 1), (ALONG, 1))
    combine((ACROSS, 0), (ALONG, 0))
    within(MID, lambda: relay(DIAGONAL, 3, 0, OUTER))
    for part in range(2):
        relay(ACROSS, 2, part)
        relay(ALONG, 2, part)
    within(MID, lambda: relay(DIAGONAL, 3, 1, OUTER))
    compute((OWN, 3), (ACROSS, 2))
    combine((DIAGONAL, 0), (OWN, 2))
    within(END, lambda: [relay(DIAGONAL, 2, part) for part in range(2)])
    compute((ALONG, 2), (DIAGONAL, 2))
    combine((ACROSS, 1), (ALONG, 1))
    combine((OWN, 3), (ACROSS, 2))
    for part in range(2):
        relay(ACROSS, 3, part)
        relay(ALONG, 3, part)
    compute((ACROSS, 3), (ALONG, 3))
    combine((ALONG, 2), (DIAGONAL, 2))
    for part in range(2):
        gather_sums(ACROSS, 2, part, TO_X)
        gather_sums(ALONG, 2, part, TO_Y)
        within(END, lambda: gather_sums(DIAGONAL, 2, part, INNER))
    within(
        END,
        lambda: [
            relay(DIAGONAL, near, part) for part in range(2) for near in (1, 3)
        ],
    )
    compute((DIAGONAL, 1), (DIAGONAL, 3))
    combine((ACROSS, 3), (ALONG, 3))
    for part in range(2):
        gather_sums(ACROSS, 3, part, TO_X)
        gather_sums(ALONG, 3, part, TO_Y)
    combine((DIAGONAL, 1), (DIAGONAL, 3))

    def end_fifth():
        for part in range(2):
            gather_sums(DIAGONAL, 3, part, INNER)
        gather_sums(DIAGONAL, 1, 0, TO_Y)
        gather_sums(DIAGONAL, 1, 1, TO_X)

    def mid_fifth():
        for part in range(2):
            gather_sums(DIAGONAL, 2, part, INNER, DIAGONAL_OUTER)

    within(END, end_fifth)
    within(MID, mid_fifth)
    down_grad(0)

    def end_sixth():
        for part in range(2):
            gather_sums(OWN, 2, part, INNER, OWN_X, OWN_Y)

    def mid_sixth():
        for part in range(2):
            gather_sums(DIAGONAL, 3, part, INNER, DIAGONAL_OUTER)
        for part in range(2):
            gather_sums(DIAGONAL, 1, part, OUTER, DIAGONAL_INNER)

    within(END, end_sixth)
    within(MID, mid_sixth)
    down_grad(1)

    def end_seventh():
        for part in range(2):
            gather_sums(OWN, 3, part, INNER, OWN_X, OWN_Y)
        gather_sums(ACROSS, 1, 0, TO_X, ACROSS_Y)
        gather_sums(ACROSS, 1, 1, TO_X)
        gather_sums(ALONG, 1, 0, TO_Y)
        gather_sums(ALONG, 1, 1, TO_Y, ALONG_X)

    def mid_seventh():
        for part in range(2):
            gather_sums(ACROSS, 1, part, TO_X)
            gather_sums(ALONG, 1, part, TO_Y)
        for part in range(2):
            gather_sums(OWN, 2, part, INNER, OWN_X, OWN_Y, OWN_OUTER)

    within(END, end_seventh)
    within(MID, mid_seventh)
    gu_grad(0)

    def diagonal_home():
        gather_sums(DIAGONAL, 0, 0, TO_Y, DIAGONAL_INNER)
        gather_sums(DIAGONAL, 0, 1, TO_X, DIAGONAL_INNER)

    def mid_eighth():
        for part in range(2):
            gather_sums(OWN, 3, part, INNER, OWN_X, OWN_Y, OWN_OUTER)

    within(MID, mid_eighth)
    diagonal_home()
    gu_grad(1)
    for part in range(2):
        within(END, lambda: gather_sums(OWN, 1, part, INNER, OWN_X, OWN_Y))
        within(MID, lambda: gather_sums(OWN, 1, part, OUTER, OWN_X, OWN_Y, OWN_INNER))
    gu_grad(2)
    gather_sums(ACROSS, 0, 1, TO_X)
    gather_sums(ALONG, 0, 0, TO_Y)
    gather_sums(ACROSS, 0, 0, TO_X, ACROSS_Y)
    gather_sums(ALONG, 0, 1, TO_Y, ALONG_X)
    gu_grad(3)

    def finish_sums(*boxes):
        gate_sums = []
        for part in range(2):
            value = part_ref[mine, core, piece(part)].astype(jnp.float32)
            for box in boxes:
                value = value + incoming(OWN, 0, part, box)
            tokens_out[piece(part), :] = value[:, :features].astype(jnp.bfloat16)
            gate_sums.append(value[:, features:])
        sums = jnp.concatenate(gate_sums, axis=0).T
        picked = jnp.zeros(routing.shape, jnp.float32)
        for index in range(experts):
            picked = jnp.where(routing == index, sums[index : index + 1], picked)
        gates_out[...] = jnp.where(usable, picked, 0.0)

    within(END, lambda: finish_sums(OWN_X, OWN_Y, OWN_INNER))
    within(MID, lambda: finish_sums(OWN_X, OWN_Y, OWN_INNER, OWN_OUTER))

    def settle(role):
        for make, args in unsent[role]:
            make(*args).wait_send()

    settle(ALL)
    within(END, lambda: settle(END))
    within(MID, lambda: settle(MID))


def finish_kernel(*refs):
    count = (len(refs) - 1) // 2
    copies = [
        pltpu.make_async_copy(refs[index], refs[count + index], refs[-1].at[index])
        for index in range(count)
    ]
    for copy in copies:
        copy.start()
    for copy in copies:
        copy.wait()


def fused_layer(tokens, grad_out, routing, replica, gates, host_expert, w_gate_up, w_down):
    count, features = tokens.shape
    owned, quarter = w_down.shape[:2]
    size = lax.axis_size("expert")
    experts = owned * size
    depth = size // 2
    chips = 4 * depth
    lanes = (experts + 127) // 128 * 128
    kind = jnp.bfloat16
    width, sums = 2 * features + lanes, features + lanes
    outside = pl.BlockSpec(memory_space=pltpu.HBM)
    inside = pl.BlockSpec(memory_space=pltpu.VMEM)
    boxes = 8 * depth * 2
    turned = (routing.shape[1], count)
    results = (
        ((count, features), kind),
        (turned, jnp.float32),
        (w_gate_up.shape, kind),
        (w_down.shape, kind),
    )
    held = pl.pallas_call(
        functools.partial(fused_kernel, experts),
        out_shape=tuple(pltpu.VMEM(*result) for result in results),
        in_specs=[outside] * 8,
        out_specs=(inside,) * 4,
        scratch_shapes=[
            pltpu.VMEM((chips, 2, count, width), kind),
            pltpu.VMEM(w_gate_up.shape, kind),
            pltpu.VMEM(w_down.shape, kind),
            pltpu.VMEM((2 * owned, chips, 2 * count, quarter), kind),
            pltpu.VMEM((owned, chips, 2 * count, quarter), kind),
            pltpu.VMEM((chips, 2, count, sums), kind),
            pltpu.VMEM((chips, count, sums), kind),
            pltpu.VMEM((boxes, count // 2, sums), kind),
            pltpu.VMEM(turned, jnp.int32),
            pltpu.VMEM(turned, jnp.int32),
            pltpu.VMEM(turned, kind),
            pltpu.SMEM(host_expert.shape, jnp.int32),
            pltpu.SemaphoreType.DMA((8,)),
            pltpu.SemaphoreType.DMA((chips, 10)),
            pltpu.SemaphoreType.DMA((chips, 2, 2)),
            pltpu.SemaphoreType.DMA((chips,)),
            pltpu.SemaphoreType.DMA((chips,)),
            pltpu.SemaphoreType.DMA((boxes,)),
            pltpu.SemaphoreType.DMA((boxes,)),
        ],
        compiler_params=pltpu.CompilerParams(
            collective_id=0, has_side_effects=True, vmem_limit_bytes=44 << 20
        ),
    )(
        *(
            pltpu.with_memory_space_constraint(value, pltpu.HBM)
            for value in (
                tokens, grad_out, routing.T, replica.T, gates.T, host_expert, w_gate_up, w_down
            )
        )
    )
    return pl.pallas_call(
        finish_kernel,
        out_shape=tuple(jax.ShapeDtypeStruct(*result) for result in results),
        in_specs=[inside] * 4,
        out_specs=(outside,) * 4,
        scratch_shapes=[pltpu.SemaphoreType.DMA((4,))],
        compiler_params=pltpu.CompilerParams(vmem_limit_bytes=1 << 20),
    )(*held)


def gathered_shards(
    tokens, grad_out, routing, replica, gates, host_expert, w_gate_up, w_down
):
    grad_tokens, grad_gates, grad_gu, grad_down = fused_layer(
        tokens, grad_out, routing, replica, gates, host_expert, w_gate_up, w_down
    )
    return (grad_tokens, grad_gates.T, grad_gu, grad_down)


def serve(tokens, grad_out, routing, replica, gates, host_expert, w_gate_up, w_down):
    grid = lax.axis_size("dp") == 4 and lax.axis_size("expert") == 8
    visits_all = routing.shape[1] >= lax.axis_size("expert")
    body = gathered_shards if grid and visits_all else shards
    return body(tokens, grad_out, routing, replica, gates, host_expert, w_gate_up, w_down)


def solution(mesh):
    in_specs = (
        P(("dp", "expert"), None),
        P(("dp", "expert"), None),
        P(("dp", "expert"), None),
        P(("dp", "expert"), None),
        P(("dp", "expert"), None),
        P(),
        P("expert", None, "dp", None),
        P("expert", "dp", None),
    )
    out_specs = (
        P(("dp", "expert"), None),
        P(("dp", "expert"), None),
        P("expert", None, "dp", None),
        P("expert", "dp", None),
    )
    return jax.shard_map(serve, mesh=mesh, in_specs=in_specs, out_specs=out_specs, check_vma=False)
```

time: 95.6 us -> 72.4 us (0.76)
  Pallas kernels: 81.7 us -> 71.4 us
  local copies, waits for them, and re-layouts: 6.97 us -> 0 us
  other arithmetic: 5.95 us -> 0 us
    pallas_call x1 -> x2, Pallas kernels: 81.7 us -> 71.4 us  [the longest x1 69.1 us: fused_layer(): pl.pallas_call(functools.partial(fused_kernel, experts), out_shape=tuple(...]
    unnamed x6 -> x0, local copies, waits for them, and re-layouts: 5.24 us -> none
    concatenate x1 -> x0, other arithmetic: 1.7 us -> none  [gathered_shards(): payload = jnp.concatenate([tokens, grad_out, side], axis=1)]
    slice x1 -> x0, local copies, waits for them, and re-layouts: 1.57 us -> none  [gathered_shards(): grad_tokens = summed[:, :features]]
    convert_element_type x2 -> x0, other arithmetic: 1.38 us -> none  [the longest x1 0.7 us: gathered_shards(): sums = summed[:, features:features + experts].astype(jnp.float32)]
    reduce_sum x2 -> x0, other arithmetic: 1.33 us -> none  [the longest x1 0.71 us: chosen_gates(): jnp.sum(jnp.where(picks, gates.astype(jnp.float32)[:, :, None], 0.0), axi...]
where the time goes in v1:
time: 72.4 us; the launch traced here: 72.2 us
  Pallas kernels  71.4 us (99%)
  between operations  0.82 us (1%)
    pallas_call x1, Pallas kernels, fused_layer(): pl.pallas_call(functools.partial(fused_kernel, experts), out_shape=tuple(...  69.1 us
    pallas_call x1, Pallas kernels, fused_layer(): pl.pallas_call(finish_kernel, out_shape=tuple((jax.ShapeDtypeStruct(*resu...  2.26 us

profile of v1, /device:TPU:0, one launch (start us, length us, event | category | flops | bytes accessed | tf_op | source)
XLA Modules:
  0.0 72.2 jit_solution(9865279267311889845)
XLA Ops:
  0.6 69.1 %shard_map.111 = (bf16[32,2048]{1,0:T(8,128)(2,1)S(1)}, f32[8,32]{1,0:T(8,128)S(1)}, bf16[2,2,192,2048]{3,2,1,0:T(8,128)(2,1)S(1)}, bf16[2,192,2048]{2,1,0:T(8,128)(2,1)S(1)}) custom-call(bf16[32,2048]{1,0:T(8,128)(2,1)} %tokens_hbm.1, bf16[32,2048]{1,0:T(8,128)(2,1)} %grad_out_hbm.1, s32[8,32]{1,0:T(8,128)} %bitcast.4, s32[8,32]{1,0:T(8,128)} %bitcast.5, ...), custom_call_target="tpu_custom_call" | custom-call | tf_op jit(solution)/shard_map/pallas_call | solution.py:791
  69.8 2.3 %shard_map.112 = (bf16[32,2048]{1,0:T(8,128)(2,1)}, f32[8,32]{1,0:T(8,128)}, bf16[2,2,192,2048]{3,2,1,0:T(8,128)(2,1)}, bf16[2,192,2048]{2,1,0:T(8,128)(2,1)}) custom-call(bf16[32,2048]{1,0:T(8,128)(2,1)S(1)} %get-tuple-element.12.refs_0_, f32[8,32]{1,0:T(8,128)S(1)} %get-tuple-element.13.refs_1_, bf16[2,2,192,2048]{3,2,1,0:T(8,128)(2,1)S(1)} %get-tuple-element.14.refs_2_, ...), custom_call_target="tpu_custom_call" | custom-call | tf_op jit(solution)/shard_map/pallas_call | solution.py:828

commit v2 on v1

--- a/solution.py
+++ b/solution.py
@@ -225,9 +225,182 @@
 
 
 OWN, ACROSS, ALONG, DIAGONAL = range(4)
-PARTNER, TO_X, TO_Y, INNER, OUTER = range(5)
-OWN_X, OWN_Y, OWN_INNER, OWN_OUTER, ACROSS_Y, ALONG_X, DIAGONAL_INNER, DIAGONAL_OUTER = range(8)
-ALL, END, MID = range(3)
+PARTNER, TO_X, TO_Y, INNER, OUTER, FAR_MID, FAR_END = range(7)
+OWN_X, OWN_Y, OWN_INNER, OWN_OUTER, OWN_FAR_MID, OWN_FAR_END = range(6)
+ACROSS_Y, ALONG_X, DIAGONAL_INNER, DIAGONAL_OUTER = range(6, 10)
+BOXES = 10
+END, MID = range(2)
+
+GROUPS = (
+    ((OWN, 0), (OWN, 1), (ACROSS, 0), (ALONG, 0),),
+    ((DIAGONAL, 0), (OWN, 2), (ACROSS, 1), (ALONG, 1),),
+    ((OWN, 3), (ACROSS, 2), (ALONG, 2), (DIAGONAL, 2),),
+    ((DIAGONAL, 3), (DIAGONAL, 1),),
+    ((ACROSS, 3), (ALONG, 3),),
+)
+ARRIVE, SEND, COMBINE, SUM = range(1, 5)
+WHOLE = 2
+
+SCHEDULE = (
+    (
+        (
+            20001, 20012, 20003, 20002, 20013, 20011, 12010, 11000, 22011, 21002,
+            10110, 20112, 20020, 10100, 20111, 13000, 12000, 20101, 10210, 13010,
+            23003, 20102, 11010, 10200, 20202, 22020, 11110, 20120, 23013, 12110,
+            21020, 20211, 20220, 20201, 20212,
+        ),
+        (
+            10300, 11100, 23020, 12100, 22120, 12200, 21102, 21120, 10310, 22111,
+        ),
+        (
+            20302,
+        ),
+        (
+            20320, 20301, 20312, 11200, 13200, 20311, 32000, 30100, 12210, 30000,
+            31000, 41010, 22220, 11210, 21220, 13210, 23220,
+        ),
+        (),
+        (),
+        (
+            13110, 31100, 12300, 13300, 32100, 13100, 30200, 42100, 23120, 41110,
+            13310, 23320, 31200, 11310, 41200, 33200, 12310, 43200, 11300, 22320,
+            32200, 42200, 41210, 42210, 21320,
+        ),
+        (),
+        (
+            43210, 33300, 43310, 43300,
+        ),
+        (
+            33100, 43100, 43110,
+        ),
+        (
+            40200, 33000, 40210, 31300, 32300, 42300, 41300, 42310, 43000, 41310,
+            41100, 43010, 30300,
+        ),
+        (
+            40300, 42110,
+        ),
+        (
+            40310, 42000, 41000, 40100,
+        ),
+        (
+            42010, 40110,
+        ),
+        (),
+        (
+            40000, 40010,
+        ),
+    ),
+    (
+        (
+            20004, 20013, 20001, 20011, 20014, 20003, 20012, 20002, 10100, 10210,
+            11000, 12010, 21002, 22011, 20103, 20214, 10110, 11010, 20101, 10200,
+            20111, 20113, 20102, 20112, 20202, 20204, 13000, 20212, 20211, 12000,
+            10300, 20201, 20304, 23003, 20120, 21020, 20220, 22020, 12100, 10310,
+            20020, 13010, 20314, 23013, 11100, 13100, 13200, 23020, 20320, 20301,
+            12110, 11110, 23204, 20311, 20302, 23103,
+        ),
+        (
+            22120, 20312, 13110, 21120, 23113, 23120, 13210, 23214,
+        ),
+        (),
+        (
+            12200, 11210, 12210, 32000, 11200, 13300, 21220, 22220, 23304, 23220,
+            30000, 42000,
+        ),
+        (
+            31000, 13310, 23314,
+        ),
+        (
+            23320, 11300,
+        ),
+        (
+            12300, 32100, 11310, 21320, 42100, 12310, 31100, 42110, 22320,
+        ),
+        (),
+        (
+            41110, 33200, 33300, 43300, 43310, 41100,
+        ),
+        (),
+        (
+            30100, 43200, 33100, 31200, 43100, 31300, 32300, 42300, 41300, 43110,
+            42310, 41310,
+        ),
+        (
+            41200, 43210, 33000, 32200, 42200, 40110, 30200, 42210, 30300, 43000,
+            40300, 40100, 41210, 40310,
+        ),
+        (
+            40200, 43010, 41000,
+        ),
+        (
+            40210, 42010, 41010,
+        ),
+        (
+            40000,
+        ),
+        (
+            40010,
+        ),
+    ),
+)
+
+
+PLACES = sum(GROUPS, ())
+SWAPPED = (1, 0, 2, 3)
+CROSSED = (2, 3, 0, 1)
+
+
+def place(role, near):
+    return PLACES.index((role, near))
+
+
+def seen_from(kind, way, role, near):
+    if way == TO_X:
+        return role ^ 1, near
+    if way == TO_Y:
+        return role ^ 2, near
+    if way == PARTNER:
+        return role, near
+    if way == FAR_MID or way == FAR_END:
+        return role, 3 - near
+    return role, (CROSSED if kind == MID and way == INNER else SWAPPED)[near]
+
+
+def within_plane(kind, near):
+    return near == 0 or near == 3 or (near == 1 and kind == END)
+
+
+def parent(kind, role, near, part):
+    if role == ACROSS:
+        return TO_X
+    if role == ALONG:
+        return TO_Y
+    if role == DIAGONAL and within_plane(kind, near):
+        return (TO_Y, TO_X)[part]
+    if role == OWN and near == 0:
+        return None
+    if near == 3:
+        return FAR_END
+    return OUTER if kind == MID and near == 1 else INNER
+
+
+def children(kind, role, near, part):
+    if role == ACROSS:
+        return (ACROSS_Y,) if part == 0 and within_plane(kind, near) else ()
+    if role == ALONG:
+        return (ALONG_X,) if part == 1 and within_plane(kind, near) else ()
+    if role == DIAGONAL:
+        if near == 0:
+            return (DIAGONAL_INNER,)
+        return (DIAGONAL_OUTER,) if kind == MID and near == 2 else ()
+    boxes = (OWN_X, OWN_Y)
+    if near == 0:
+        boxes += (OWN_INNER,)
+        boxes += (OWN_FAR_MID, OWN_FAR_END) if kind == END else (OWN_OUTER,)
+    if near == 2 and kind == MID:
+        boxes += (OWN_OUTER,)
+    return boxes
 
 
 def usable_choices(routing, replica, host_ref):
@@ -259,6 +432,7 @@
     part_ref,
     paired_ref,
     inbox_ref,
+    gate_sums_ref,
     routing_ref,
     replica_ref,
     gates_ref,
@@ -280,17 +454,12 @@
     half = count // 2
     features = tokens_hbm.shape[1]
     lanes = rows_ref.shape[3] - 2 * features
-    owned, quarter = down_ref.shape[:2]
+    owned, quarter = down_hbm.shape[:2]
+    hidden_units = owned * quarter
     across = row * 2 + 1 - column
     along = (1 - row) * 2 + column
-    roles = (dp, across, along, (1 - row) * 2 + 1 - column)
     upper = height // (depth // 2)
-    levels = (
-        height,
-        height + 1 - 2 * (height % 2),
-        depth // 2 - upper,
-        (depth - 1) * (1 - upper),
-    )
+    outer_level = height + 1 - 2 * (height % 2)
     is_mid = (height + upper) % 2 == 1
     is_end = (height + upper) % 2 == 0
     inner_level = height + 1 - 2 * upper
@@ -299,28 +468,28 @@
         (across, expert),
         (along, expert),
         (dp, inner_level * 2 + core),
-        (dp, levels[1] * 2 + core),
-    )
-    scope = [ALL]
-    unsent = ([], [], [])
-
-    def within(role, body):
-        scope[0] = role
-
-        @pl.when(is_end if role == END else is_mid)
+        (dp, outer_level * 2 + core),
+        (dp, (depth // 2 - upper) * 2 + core),
+        (dp, (depth - 1) * (1 - upper) * 2 + core),
+    )
+    kinds = [None]
+    unsent = ([], [])
+    shared = []
+
+    def within(kind, body):
+        kinds[0] = kind
+
+        @pl.when(is_end if kind == END else is_mid)
         def _():
             body()
 
-        scope[0] = ALL
+        kinds[0] = None
 
     def begin(make, *args):
         make(*args).start()
-        unsent[scope[0]].append((make, args))
-
-    def chip(role, near):
-        return roles[role] * depth + levels[near]
-
-    mine = chip(OWN, 0)
+        (shared if kinds[0] is None else unsent[kinds[0]]).append((make, args))
+
+    mine = place(OWN, 0)
     loads = [
         pltpu.make_async_copy(routing_hbm, routing_ref, local.at[0]),
         pltpu.make_async_copy(replica_hbm, replica_ref, local.at[1]),
@@ -330,18 +499,34 @@
         pltpu.make_async_copy(
             grad_out_hbm, rows_ref.at[mine, core, :, pl.ds(features, features)], local.at[5]
         ),
-        pltpu.make_async_copy(gu_hbm, gu_ref, local.at[6]),
-        pltpu.make_async_copy(down_hbm, down_ref, local.at[7]),
     ]
+    for index in range(2 * owned):
+        loads.append(
+            pltpu.make_async_copy(
+                gu_hbm.at[index % owned, index // owned],
+                gu_ref.at[pl.ds(index * quarter, quarter)],
+                local.at[6 + index],
+            )
+        )
+    for index in range(owned):
+        loads.append(
+            pltpu.make_async_copy(
+                down_hbm.at[index],
+                down_ref.at[pl.ds(index * quarter, quarter)],
+                local.at[6 + 2 * owned + index],
+            )
+        )
     for load in loads:
         load.start()
     barrier = pltpu.get_barrier_semaphore()
-    for way in (PARTNER, TO_X, TO_Y, INNER):
-        pl.semaphore_signal(barrier, inc=1, device_id=targets_of[way], device_id_type=MESH)
-
-    @pl.when(is_mid)
-    def _():
-        pl.semaphore_signal(barrier, inc=1, device_id=targets_of[OUTER], device_id_type=MESH)
+    for kind, ways in ((END, (FAR_MID,)), (MID, (OUTER,))):
+
+        @pl.when(is_end if kind == END else is_mid)
+        def _():
+            for way in (PARTNER, TO_X, TO_Y, INNER, FAR_END) + ways:
+                pl.semaphore_signal(
+                    barrier, inc=1, device_id=targets_of[way], device_id_type=MESH
+                )
 
     for load in loads[:4]:
         load.wait()
@@ -359,39 +544,26 @@
     rows_ref[mine, core, :, 2 * features :] = weights.T.astype(jnp.bfloat16)
     for load in loads[4:6]:
         load.wait()
-    pl.semaphore_wait(barrier, 4 + is_mid.astype(jnp.int32))
+    pl.semaphore_wait(barrier, 6)
 
     def piece(part):
         return pl.ds(part * half, half)
 
     def row_copy(role, near, part, way):
-        at = chip(role, near)
-        block = rows_ref.at[at, core] if part is None else rows_ref.at[at, core, piece(part)]
+        at, to = place(role, near), place(*seen_from(kinds[0], way, role, near))
+        span = slice(None) if part is None else piece(part)
         index = 0 if part is None else part
         return pltpu.make_async_remote_copy(
-            src_ref=block,
-            dst_ref=block,
+            src_ref=rows_ref.at[at, core, span],
+            dst_ref=rows_ref.at[to, core, span],
             send_sem=sent.at[at, way * 2 + index],
-            recv_sem=landed.at[at, core, index],
+            recv_sem=landed.at[to, core, index],
             device_id=targets_of[way],
             device_id_type=MESH,
         )
 
-    def forward(role, near, part, *ways):
-        for way in ways:
-            begin(row_copy, role, near, part, way)
-
-    def arrive(role, near, part):
-        row_copy(role, near, part, PARTNER).wait_recv()
-
-    def relay(role, near, part, *ways):
-        arrive(role, near, part)
-        forward(role, near, part, *ways)
-        if part == 1:
-            forward(role, near, None, PARTNER)
-
     def partner_rows(role, near):
-        at = chip(role, near)
+        at = place(role, near)
         block = rows_ref.at[at, 1 - core]
         pltpu.make_async_remote_copy(
             src_ref=block,
@@ -424,336 +596,193 @@
             device_id_type=MESH,
         )
 
-    def compute(*group):
-        chips = [chip(role, near) for role, near in group]
-        for role, near in group:
+    def stacked(ref, index, first, size):
+        group = GROUPS[index]
+        start = place(*group[0])
+        rows = ref[start : start + len(group), ..., first : first + size]
+        return rows.reshape(len(group) * chip_rows, size)
+
+    def keep(ref, index, first, values):
+        start, stop = place(*GROUPS[index][0]), place(*GROUPS[index][-1]) + 1
+        size = values.shape[1]
+        shape = (stop - start,) + ref.shape[1:-1] + (size,)
+        ref[start:stop, ..., first : first + size] = values.reshape(shape)
+
+    def ahead(group):
+        for role, near in GROUPS[group]:
             partner_rows(role, near)
-
-        def take(first, size):
-            return jnp.concatenate(
-                [
-                    rows_ref[at, :, :, first : first + size].reshape(chip_rows, size)
-                    for at in chips
-                ],
-                axis=0,
+        side = stacked(rows_ref, group, 2 * features, lanes).astype(jnp.float32)
+        slots = lax.broadcasted_iota(jnp.int32, side.shape, 1)
+        shape = (side.shape[0], hidden_units)
+        units = lax.broadcasted_iota(jnp.int32, shape, 1)
+        at_expert = [slots == expert * owned + index for index in range(owned)]
+        of_expert = [
+            (units >= index * quarter) & (units < (index + 1) * quarter) for index in range(owned)
+        ]
+        weight = jnp.zeros(shape, jnp.float32)
+        for index in range(owned):
+            scale = jnp.sum(jnp.where(at_expert[index], side, 0.0), axis=1, keepdims=True)
+            weight = jnp.where(of_expert[index], scale, weight)
+        mixed = rows_by_columns(stacked(rows_ref, group, 0, features), gu_ref[...])
+        raw_hidden = rows_by_columns(stacked(rows_ref, group, features, features), down_ref[...])
+        gate_pre = mixed[:, :hidden_units]
+        up_part = mixed[:, hidden_units:]
+        sigmoid_gate = jax.nn.sigmoid(gate_pre)
+        active = gate_pre * sigmoid_gate
+        hidden = (active * up_part).astype(jnp.bfloat16).astype(jnp.float32)
+        gate_parts = hidden * raw_hidden
+        gate_side = jnp.zeros(side.shape, jnp.float32)
+        for index in range(owned):
+            total = jnp.sum(
+                jnp.where(of_expert[index], gate_parts, 0.0), axis=1, keepdims=True
             )
-
-        inputs = take(0, features)
-        upstream = take(features, features)
-        side = take(2 * features, lanes).astype(jnp.float32)
-        slots = lax.broadcasted_iota(jnp.int32, side.shape, 1)
-        gate_side = jnp.zeros(side.shape, jnp.float32)
-        grads = []
-        for local_expert in range(owned):
-            at_expert = slots == expert * owned + local_expert
-            weight = jnp.sum(jnp.where(at_expert, side, 0.0), axis=1, keepdims=True)
-            gate_pre = rows_by_columns(inputs, gu_ref[local_expert, 0])
-            up_part = rows_by_columns(inputs, gu_ref[local_expert, 1])
-            raw_hidden = rows_by_columns(upstream, down_ref[local_expert])
-            sigmoid_gate = jax.nn.sigmoid(gate_pre)
-            active = gate_pre * sigmoid_gate
-            hidden = (active * up_part).astype(jnp.bfloat16).astype(jnp.float32)
-            gate_part = jnp.sum(hidden * raw_hidden, axis=1, keepdims=True)
-            gate_side = jnp.where(at_expert, gate_part, gate_side)
-            grad_hidden = raw_hidden * weight
-            grad_gate = (
-                grad_hidden * up_part * sigmoid_gate * (1.0 + gate_pre * (1.0 - sigmoid_gate))
-            )
-            weighted = (hidden * weight).astype(jnp.bfloat16)
-            grads.append(grad_gate.astype(jnp.bfloat16))
-            grads.append((grad_hidden * active).astype(jnp.bfloat16))
-            for index, at in enumerate(chips):
-                span = slice(index * chip_rows, (index + 1) * chip_rows)
-                hidden_ref[local_expert, at] = weighted[span]
-                mixed_ref[2 * local_expert, at] = grads[-2][span]
-                mixed_ref[2 * local_expert + 1, at] = grads[-1][span]
-        dx = jnp.zeros(inputs.shape, jnp.float32)
-        for index in range(2 * owned):
-            dx = dx + jnp.dot(
-                grads[index],
-                gu_ref[index // 2, index % 2],
-                preferred_element_type=jnp.float32,
-            )
-        for index, at in enumerate(chips):
-            span = slice(index * chip_rows, (index + 1) * chip_rows)
-            part_ref[at, :, :, :features] = (
-                dx[span].astype(jnp.bfloat16).reshape(2, count, features)
-            )
-            part_ref[at, :, :, features:] = (
-                gate_side[span].astype(jnp.bfloat16).reshape(2, count, lanes)
-            )
-            begin(pair_copy, at)
-
-    def combine(*group):
-        for role, near in group:
-            at = chip(role, near)
-            pair_copy(at).wait_recv()
-            part_ref[at, core] = (
-                part_ref[at, core].astype(jnp.float32) + paired_ref[at].astype(jnp.float32)
-            ).astype(jnp.bfloat16)
-
-    def box_index(box, role, near, part):
-        return (box * depth + levels[near]) * 2 + part
+            gate_side = jnp.where(at_expert[index], total, gate_side)
+        grad_hidden = raw_hidden * weight
+        grad_gate = (
+            grad_hidden * up_part * sigmoid_gate * (1.0 + gate_pre * (1.0 - sigmoid_gate))
+        ).astype(jnp.bfloat16)
+        grad_up = (grad_hidden * active).astype(jnp.bfloat16)
+        weighted = (hidden * weight).astype(jnp.bfloat16)
+        gate_side = gate_side.astype(jnp.bfloat16)
+        keep(hidden_ref, group, 0, weighted)
+        keep(mixed_ref, group, 0, grad_gate)
+        keep(mixed_ref, group, hidden_units, grad_up)
+        keep(part_ref, group, features, gate_side)
+
+    def back(group):
+        dx = jnp.dot(
+            stacked(mixed_ref, group, 0, 2 * hidden_units),
+            gu_ref[...],
+            preferred_element_type=jnp.float32,
+        )
+        keep(part_ref, group, 0, dx.astype(jnp.bfloat16))
+        for role, near in GROUPS[group]:
+            begin(pair_copy, place(role, near))
+
+    def combine(role, near):
+        at = place(role, near)
+        pair_copy(at).wait_recv()
+        part_ref[at, core] = (
+            part_ref[at, core].astype(jnp.float32) + paired_ref[at].astype(jnp.float32)
+        ).astype(jnp.bfloat16)
+
+    def box_index(box, near, part):
+        return (box * depth + near) * 2 + part
 
     def sum_copy(role, near, part, way, box):
-        index = box_index(box, role, near, part)
+        index = box_index(box, seen_from(kinds[0], way, role, near)[1], part)
         return pltpu.make_async_remote_copy(
-            src_ref=part_ref.at[chip(role, near), core, piece(part)],
+            src_ref=part_ref.at[place(role, near), core, piece(part)],
             dst_ref=inbox_ref.at[index],
-            send_sem=sums_sent.at[index],
+            send_sem=sums_sent.at[box_index(box, near, part)],
             recv_sem=sums_landed.at[index],
             device_id=targets_of[way],
             device_id_type=MESH,
         )
 
     def incoming(role, near, part, box):
-        index = box_index(box, role, near, part)
-        sum_copy(role, near, part, PARTNER, box).wait_recv()
+        index = box_index(box, near, part)
+        pltpu.make_async_remote_copy(
+            src_ref=inbox_ref.at[index],
+            dst_ref=inbox_ref.at[index],
+            send_sem=sums_sent.at[index],
+            recv_sem=sums_landed.at[index],
+            device_id=targets_of[PARTNER],
+            device_id_type=MESH,
+        ).wait_recv()
         return inbox_ref[index].astype(jnp.float32)
 
-    def send_sum(role, near, part, way):
+    def home_box(role, way):
         if way == TO_X:
-            box = ALONG_X if role == DIAGONAL else OWN_X
-        elif way == TO_Y:
-            box = ACROSS_Y if role == DIAGONAL else OWN_Y
-        else:
-            outward = way == INNER and scope[0] == END
-            box = (OWN_OUTER if outward else OWN_INNER) if role == OWN else (
-                DIAGONAL_OUTER if outward else DIAGONAL_INNER
-            )
-        begin(sum_copy, role, near, part, way, box)
-
-    def gather_sums(role, near, part, way, *boxes):
-        at = chip(role, near)
+            return ALONG_X if role == DIAGONAL else OWN_X
+        if way == TO_Y:
+            return ACROSS_Y if role == DIAGONAL else OWN_Y
+        if way == FAR_END:
+            return OWN_FAR_END if kinds[0] == END else OWN_FAR_MID
+        if kinds[0] == END:
+            return OWN_OUTER if role == OWN else DIAGONAL_OUTER
+        return OWN_INNER if role == OWN else DIAGONAL_INNER
+
+    def gather_sums(role, near, part):
+        kind = kinds[0]
+        at = place(role, near)
+        boxes, way = children(kind, role, near, part), parent(kind, role, near, part)
         if boxes:
             value = part_ref[at, core, piece(part)].astype(jnp.float32)
             for box in boxes:
                 value = value + incoming(role, near, part, box)
-            part_ref[at, core, piece(part)] = value.astype(jnp.bfloat16)
-        send_sum(role, near, part, way)
+            if way is None:
+                tokens_out[piece(part), :] = value[:, :features].astype(jnp.bfloat16)
+                gate_sums_ref[piece(part), :] = value[:, features:]
+            else:
+                part_ref[at, core, piece(part)] = value.astype(jnp.bfloat16)
+        if way is not None:
+            begin(sum_copy, role, near, part, way, home_box(role, way))
 
     total_rows = 4 * depth * chip_rows
 
-    def down_grad(local_expert):
-        upstream = rows_ref[:, :, :, features : 2 * features].reshape(total_rows, features)
-        weighted = hidden_ref[local_expert].reshape(total_rows, quarter)
-        grad_down_ref[local_expert] = columns_by_columns(weighted, upstream)
-
-    def gu_grad(index):
-        inputs = rows_ref[:, :, :, :features].reshape(total_rows, features)
-        grads = mixed_ref[index].reshape(total_rows, quarter)
-        grad_gu_ref[index // 2, index % 2] = columns_by_columns(grads, inputs)
-
-    forward(OWN, 0, 0, INNER, TO_X, TO_Y)
-    within(MID, lambda: forward(OWN, 0, 0, OUTER))
-    forward(OWN, 0, 1, INNER, TO_X, TO_Y)
-    within(MID, lambda: forward(OWN, 0, 1, OUTER))
-    forward(OWN, 0, None, PARTNER)
-
-    def end_first():
-        relay(ACROSS, 0, 0, TO_Y)
-        relay(OWN, 1, 0, TO_X, TO_Y)
-        relay(ALONG, 0, 0)
-        relay(ALONG, 0, 1, TO_X)
-        relay(OWN, 1, 1, TO_X, TO_Y)
-        relay(ACROSS, 0, 1)
-
-    def mid_first():
-        relay(OWN, 1, 0, INNER, TO_X)
-        relay(OWN, 2, 0, OUTER)
-        relay(ACROSS, 0, 0, TO_Y)
-        forward(OWN, 1, 0, TO_Y)
-        relay(ALONG, 0, 0)
-        relay(OWN, 1, 1, INNER)
-        relay(OWN, 2, 1, OUTER)
-        relay(ALONG, 0, 1, TO_X)
-        forward(OWN, 1, 1, TO_X, TO_Y)
-        relay(ACROSS, 0, 1)
-        forward(OWN, 2, 0, TO_X, TO_Y)
-        forward(OWN, 2, 1, TO_X, TO_Y)
-
-    within(END, end_first)
-    within(MID, mid_first)
-    for load in loads[6:]:
-        load.wait()
-    compute((OWN, 0), (OWN, 1))
-
-    def end_second():
-        relay(DIAGONAL, 0, 0, INNER)
-        relay(OWN, 2, 0, TO_X, TO_Y)
-        relay(DIAGONAL, 0, 1, INNER)
-        relay(OWN, 2, 1, TO_X, TO_Y)
-
-    def mid_second():
-        relay(OWN, 3, 0, OUTER)
-        relay(DIAGONAL, 0, 0, INNER)
-        relay(OWN, 3, 1, OUTER)
-        relay(DIAGONAL, 0, 1, INNER)
-        forward(OWN, 3, 0, TO_X, TO_Y)
-        forward(OWN, 3, 1, TO_X, TO_Y)
-
-    within(END, end_second)
-    within(MID, mid_second)
-    compute((ACROSS, 0), (ALONG, 0))
-
-    def end_third():
-        relay(ACROSS, 1, 0)
-        relay(ALONG, 1, 0)
-        relay(OWN, 3, 0, TO_X, TO_Y)
-
-    def mid_third():
-        relay(ACROSS, 1, 0)
-        relay(ALONG, 1, 0)
-        relay(DIAGONAL, 1, 0, INNER)
-        relay(DIAGONAL, 2, 0, OUTER)
-
-    within(END, end_third)
-    within(MID, mid_third)
-    compute((DIAGONAL, 0), (OWN, 2))
-    combine((OWN, 0), (OWN, 1))
-
-    def end_fourth():
-        relay(ACROSS, 1, 1)
-        relay(ALONG, 1, 1)
-        relay(OWN, 3, 1, TO_X, TO_Y)
-        forward(ACROSS, 1, 0, TO_Y)
-        forward(ALONG, 1, 1, TO_X)
-
-    def mid_fourth():
-        relay(DIAGONAL, 1, 1, INNER)
-        relay(DIAGONAL, 2, 1, OUTER)
-        relay(ACROSS, 1, 1)
-        relay(ALONG, 1, 1)
-
-    within(END, end_fourth)
-    within(MID, mid_fourth)
-    compute((ACROSS, 1), (ALONG, 1))
-    combine((ACROSS, 0), (ALONG, 0))
-    within(MID, lambda: relay(DIAGONAL, 3, 0, OUTER))
-    for part in range(2):
-        relay(ACROSS, 2, part)
-        relay(ALONG, 2, part)
-    within(MID, lambda: relay(DIAGONAL, 3, 1, OUTER))
-    compute((OWN, 3), (ACROSS, 2))
-    combine((DIAGONAL, 0), (OWN, 2))
-    within(END, lambda: [relay(DIAGONAL, 2, part) for part in range(2)])
-    compute((ALONG, 2), (DIAGONAL, 2))
-    combine((ACROSS, 1), (ALONG, 1))
-    combine((OWN, 3), (ACROSS, 2))
-    for part in range(2):
-        relay(ACROSS, 3, part)
-        relay(ALONG, 3, part)
-    compute((ACROSS, 3), (ALONG, 3))
-    combine((ALONG, 2), (DIAGONAL, 2))
-    for part in range(2):
-        gather_sums(ACROSS, 2, part, TO_X)
-        gather_sums(ALONG, 2, part, TO_Y)
-        within(END, lambda: gather_sums(DIAGONAL, 2, part, INNER))
-    within(
-        END,
-        lambda: [
-            relay(DIAGONAL, near, part) for part in range(2) for near in (1, 3)
-        ],
-    )
-    compute((DIAGONAL, 1), (DIAGONAL, 3))
-    combine((ACROSS, 3), (ALONG, 3))
-    for part in range(2):
-        gather_sums(ACROSS, 3, part, TO_X)
-        gather_sums(ALONG, 3, part, TO_Y)
-    combine((DIAGONAL, 1), (DIAGONAL, 3))
-
-    def end_fifth():
-        for part in range(2):
-            gather_sums(DIAGONAL, 3, part, INNER)
-        gather_sums(DIAGONAL, 1, 0, TO_Y)
-        gather_sums(DIAGONAL, 1, 1, TO_X)
-
-    def mid_fifth():
-        for part in range(2):
-            gather_sums(DIAGONAL, 2, part, INNER, DIAGONAL_OUTER)
-
-    within(END, end_fifth)
-    within(MID, mid_fifth)
-    down_grad(0)
-
-    def end_sixth():
-        for part in range(2):
-            gather_sums(OWN, 2, part, INNER, OWN_X, OWN_Y)
-
-    def mid_sixth():
-        for part in range(2):
-            gather_sums(DIAGONAL, 3, part, INNER, DIAGONAL_OUTER)
-        for part in range(2):
-            gather_sums(DIAGONAL, 1, part, OUTER, DIAGONAL_INNER)
-
-    within(END, end_sixth)
-    within(MID, mid_sixth)
-    down_grad(1)
-
-    def end_seventh():
-        for part in range(2):
-            gather_sums(OWN, 3, part, INNER, OWN_X, OWN_Y)
-        gather_sums(ACROSS, 1, 0, TO_X, ACROSS_Y)
-        gather_sums(ACROSS, 1, 1, TO_X)
-        gather_sums(ALONG, 1, 0, TO_Y)
-        gather_sums(ALONG, 1, 1, TO_Y, ALONG_X)
-
-    def mid_seventh():
-        for part in range(2):
-            gather_sums(ACROSS, 1, part, TO_X)
-            gather_sums(ALONG, 1, part, TO_Y)
-        for part in range(2):
-            gather_sums(OWN, 2, part, INNER, OWN_X, OWN_Y, OWN_OUTER)
-
-    within(END, end_seventh)
-    within(MID, mid_seventh)
-    gu_grad(0)
-
-    def diagonal_home():
-        gather_sums(DIAGONAL, 0, 0, TO_Y, DIAGONAL_INNER)
-        gather_sums(DIAGONAL, 0, 1, TO_X, DIAGONAL_INNER)
-
-    def mid_eighth():
-        for part in range(2):
-            gather_sums(OWN, 3, part, INNER, OWN_X, OWN_Y, OWN_OUTER)
-
-    within(MID, mid_eighth)
-    diagonal_home()
-    gu_grad(1)
-    for part in range(2):
-        within(END, lambda: gather_sums(OWN, 1, part, INNER, OWN_X, OWN_Y))
-        within(MID, lambda: gather_sums(OWN, 1, part, OUTER, OWN_X, OWN_Y, OWN_INNER))
-    gu_grad(2)
-    gather_sums(ACROSS, 0, 1, TO_X)
-    gather_sums(ALONG, 0, 0, TO_Y)
-    gather_sums(ACROSS, 0, 0, TO_X, ACROSS_Y)
-    gather_sums(ALONG, 0, 1, TO_Y, ALONG_X)
-    gu_grad(3)
-
-    def finish_sums(*boxes):
-        gate_sums = []
-        for part in range(2):
-            value = part_ref[mine, core, piece(part)].astype(jnp.float32)
-            for box in boxes:
-                value = value + incoming(OWN, 0, part, box)
-            tokens_out[piece(part), :] = value[:, :features].astype(jnp.bfloat16)
-            gate_sums.append(value[:, features:])
-        sums = jnp.concatenate(gate_sums, axis=0).T
-        picked = jnp.zeros(routing.shape, jnp.float32)
-        for index in range(experts):
-            picked = jnp.where(routing == index, sums[index : index + 1], picked)
-        gates_out[...] = jnp.where(usable, picked, 0.0)
-
-    within(END, lambda: finish_sums(OWN_X, OWN_Y, OWN_INNER))
-    within(MID, lambda: finish_sums(OWN_X, OWN_Y, OWN_INNER, OWN_OUTER))
-
-    def settle(role):
-        for make, args in unsent[role]:
+    def weight_grad(ref, out_ref, source, first, size):
+        sources = rows_ref[:, :, :, source * features : (source + 1) * features]
+        grads = columns_by_columns(
+            ref[:, :, first : first + size].reshape(total_rows, size),
+            sources.reshape(total_rows, features),
+        )
+        start = first
+        while start < first + size:
+            index, offset = start // quarter, start % quarter
+            taken = min(quarter - offset, first + size - start)
+            where = (index % owned, index // owned) if source == 0 else (index,)
+            out_ref[where + (pl.ds(offset, taken),)] = grads[start - first : start - first + taken]
+            start += taken
+
+    jobs = []
+    for first in range(0, 2 * hidden_units, 256):
+        size = min(256, 2 * hidden_units - first)
+        jobs.append((mixed_ref, grad_gu_ref, 0, first, size))
+    for first in range(0, hidden_units, 256):
+        size = min(256, hidden_units - first)
+        jobs.append((hidden_ref, grad_down_ref, 1, first, size))
+
+    def play(codes):
+        for code in codes:
+            action, role, near, part, way = (code // 10**place_of % 10 for place_of in range(4, -1, -1))
+            part = None if part == WHOLE else part
+            if action == ARRIVE:
+                row_copy(role, near, part, PARTNER).wait_recv()
+            elif action == SEND:
+                begin(row_copy, role, near, part, way)
+            elif action == COMBINE:
+                combine(role, near)
+            else:
+                gather_sums(role, near, part)
+
+    stages = []
+    for group in range(len(GROUPS)):
+        stages.append((ahead, (group,)))
+        stages.append((back, (group,)))
+    stages += [(weight_grad, job) for job in jobs]
+    for index, codes in enumerate(zip(*SCHEDULE, strict=True)):
+        for kind in (END, MID):
+            if codes[kind]:
+                within(kind, functools.partial(play, codes[kind]))
+        if index == 0:
+            for load in loads[6:]:
+                load.wait()
+        if index < len(stages):
+            stages[index][0](*stages[index][1])
+    sums = gate_sums_ref[...].T
+    picked = jnp.zeros(routing.shape, jnp.float32)
+    for index in range(experts):
+        picked = jnp.where(routing == index, sums[index : index + 1], picked)
+    gates_out[...] = jnp.where(usable, picked, 0.0)
+
+    def settle(sends):
+        for make, args in sends:
             make(*args).wait_send()
 
-    settle(ALL)
-    within(END, lambda: settle(END))
-    within(MID, lambda: settle(MID))
+    settle(shared)
+    within(END, lambda: settle(unsent[END]))
+    within(MID, lambda: settle(unsent[MID]))
 
 
 def finish_kernel(*refs):
@@ -780,7 +809,8 @@
     width, sums = 2 * features + lanes, features + lanes
     outside = pl.BlockSpec(memory_space=pltpu.HBM)
     inside = pl.BlockSpec(memory_space=pltpu.VMEM)
-    boxes = 8 * depth * 2
+    boxes = BOXES * depth * 2
+    units = owned * quarter
     turned = (routing.shape[1], count)
     results = (
         ((count, features), kind),
@@ -795,19 +825,20 @@
         out_specs=(inside,) * 4,
         scratch_shapes=[
             pltpu.VMEM((chips, 2, count, width), kind),
-            pltpu.VMEM(w_gate_up.shape, kind),
-            pltpu.VMEM(w_down.shape, kind),
-            pltpu.VMEM((2 * owned, chips, 2 * count, quarter), kind),
-            pltpu.VMEM((owned, chips, 2 * count, quarter), kind),
+            pltpu.VMEM((2 * units, features), kind),
+            pltpu.VMEM((units, features), kind),
+            pltpu.VMEM((chips, 2 * count, 2 * units), kind),
+            pltpu.VMEM((chips, 2 * count, units), kind),
             pltpu.VMEM((chips, 2, count, sums), kind),
             pltpu.VMEM((chips, count, sums), kind),
             pltpu.VMEM((boxes, count // 2, sums), kind),
+            pltpu.VMEM((count, lanes), jnp.float32),
             pltpu.VMEM(turned, jnp.int32),
             pltpu.VMEM(turned, jnp.int32),
             pltpu.VMEM(turned, kind),
             pltpu.SMEM(host_expert.shape, jnp.int32),
-            pltpu.SemaphoreType.DMA((8,)),
-            pltpu.SemaphoreType.DMA((chips, 10)),
+            pltpu.SemaphoreType.DMA((6 + 3 * owned,)),
+            pltpu.SemaphoreType.DMA((chips, 14)),
             pltpu.SemaphoreType.DMA((chips, 2, 2)),
             pltpu.SemaphoreType.DMA((chips,)),
             pltpu.SemaphoreType.DMA((chips,)),

time: 72.4 us -> 64.7 us (0.89)
  Pallas kernels: 71.4 us -> 63.7 us
    pallas_call x1, Pallas kernels: 69.1 us -> 61.5 us  [fused_layer(): pl.pallas_call(functools.partial(fused_kernel, experts), out_shape=tuple(...]
where the time goes in v2:
time: 64.7 us; the launch traced here: 64.6 us
  Pallas kernels  63.7 us (98%)
  between operations  0.8 us (1%)
    pallas_call x1, Pallas kernels, fused_layer(): pl.pallas_call(functools.partial(fused_kernel, experts), out_shape=tuple(...  61.5 us
    pallas_call x1, Pallas kernels, fused_layer(): pl.pallas_call(finish_kernel, out_shape=tuple((jax.ShapeDtypeStruct(*resu...  2.26 us

profile of v2, /device:TPU:0, one launch (start us, length us, event | category | flops | bytes accessed | tf_op | source)
XLA Modules:
  0.0 64.6 jit_solution(2907204254394659649)
XLA Ops:
  0.6 61.5 %shard_map.111 = (bf16[32,2048]{1,0:T(8,128)(2,1)S(1)}, f32[8,32]{1,0:T(8,128)S(1)}, bf16[2,2,192,2048]{3,2,1,0:T(8,128)(2,1)S(1)}, bf16[2,192,2048]{2,1,0:T(8,128)(2,1)S(1)}) custom-call(bf16[32,2048]{1,0:T(8,128)(2,1)} %tokens_hbm.1, bf16[32,2048]{1,0:T(8,128)(2,1)} %grad_out_hbm.1, s32[8,32]{1,0:T(8,128)} %bitcast.4, s32[8,32]{1,0:T(8,128)} %bitcast.5, ...), custom_call_target="tpu_custom_call" | custom-call | tf_op jit(solution)/shard_map/pallas_call | solution.py:821
  62.1 2.3 %shard_map.112 = (bf16[32,2048]{1,0:T(8,128)(2,1)}, f32[8,32]{1,0:T(8,128)}, bf16[2,2,192,2048]{3,2,1,0:T(8,128)(2,1)}, bf16[2,192,2048]{2,1,0:T(8,128)(2,1)}) custom-call(bf16[32,2048]{1,0:T(8,128)(2,1)S(1)} %get-tuple-element.12.refs_0_, f32[8,32]{1,0:T(8,128)S(1)} %get-tuple-element.13.refs_1_, bf16[2,2,192,2048]{3,2,1,0:T(8,128)(2,1)S(1)} %get-tuple-element.14.refs_2_, ...), custom_call_target="tpu_custom_call" | custom-call | tf_op jit(solution)/shard_map/pallas_call | solution.py:859

commit v3 on v2

--- a/solution.py
+++ b/solution.py
@@ -227,8 +227,9 @@
 OWN, ACROSS, ALONG, DIAGONAL = range(4)
 PARTNER, TO_X, TO_Y, INNER, OUTER, FAR_MID, FAR_END = range(7)
 OWN_X, OWN_Y, OWN_INNER, OWN_OUTER, OWN_FAR_MID, OWN_FAR_END = range(6)
-ACROSS_Y, ALONG_X, DIAGONAL_INNER, DIAGONAL_OUTER = range(6, 10)
-BOXES = 10
+ACROSS_Y, ALONG_X, ACROSS_OUTER, ALONG_OUTER, DIAGONAL_INNER, DIAGONAL_OUTER = range(6, 12)
+BOXES = 12
+OUTER_BOXES = (OWN_OUTER, ACROSS_OUTER, ALONG_OUTER, DIAGONAL_OUTER)
 END, MID = range(2)
 
 GROUPS = (
@@ -244,103 +245,101 @@
 SCHEDULE = (
     (
         (
-            20001, 20012, 20003, 20002, 20013, 20011, 12010, 11000, 22011, 21002,
-            10110, 20112, 20020, 10100, 20111, 13000, 12000, 20101, 10210, 13010,
-            23003, 20102, 11010, 10200, 20202, 22020, 11110, 20120, 23013, 12110,
-            21020, 20211, 20220, 20201, 20212,
-        ),
-        (
-            10300, 11100, 23020, 12100, 22120, 12200, 21102, 21120, 10310, 22111,
-        ),
-        (
-            20302,
-        ),
-        (
-            20320, 20301, 20312, 11200, 13200, 20311, 32000, 30100, 12210, 30000,
-            31000, 41010, 22220, 11210, 21220, 13210, 23220,
+            20001, 20020, 20003, 20012, 20013, 20011, 20002, 12010, 11000, 22011,
+            21002, 10100, 11010, 20101, 20102, 13000, 10110, 12000, 21020, 20112,
+            13010, 10210, 20120, 20111, 23013, 20212, 20211, 22020, 23020, 23003,
+            10200, 12100, 20220, 20201,
+        ),
+        (
+            12110, 22120, 20202, 11100, 11110, 21120,
+        ),
+        (
+            22111,
+        ),
+        (
+            10310, 20311, 12210, 21102, 10300, 20302, 30100, 32000, 20312,
+        ),
+        (
+            20301, 20320, 11200, 40110, 31100, 42000, 11210, 12200, 22220, 31000,
+            21220, 32100, 13200, 42100, 13210, 23220, 13110, 13100, 41110, 41100,
+        ),
+        (),
+        (
+            33000, 23120, 30000, 30300, 11310, 42110, 31200, 13310, 41200, 32200,
+            13300, 23320, 42200, 11300, 41010, 21320, 42210, 12300, 30200, 12310,
+            33200, 22320, 41210, 43210, 43200,
+        ),
+        (),
+        (
+            40200, 33300, 43300, 43310, 33100, 43110,
+        ),
+        (),
+        (
+            43100, 40210, 31300, 41300, 32300, 42300, 42310, 41310,
+        ),
+        (
+            43010, 43000, 40300,
+        ),
+        (
+            40310,
+        ),
+        (
+            40100, 42010, 41000,
+        ),
+        (),
+        (
+            40000, 40010,
+        ),
+    ),
+    (
+        (
+            20014, 20001, 20013, 20012, 20020, 20003, 20002, 20004, 20011, 11000,
+            10210, 12010, 10100, 22011, 20103, 21002, 20214, 10200, 10110, 12000,
+            20112, 20101, 20204, 11010, 20111, 21020, 20113, 20102, 20202, 20201,
+            22020, 10300, 20304, 20120, 13000, 13010, 23003,
+        ),
+        (
+            23013, 20220, 20212, 20302, 23020, 10310, 20314, 11100,
+        ),
+        (
+            20211, 11110, 21120, 12100, 12110, 20301, 13110, 13200, 22120, 31000,
+            30000, 23113, 20320, 23204,
+        ),
+        (
+            13210, 13100, 23220, 12200, 23103, 23214, 20311,
+        ),
+        (
+            20312, 11210, 11200, 21220, 12210, 30100, 13310, 22220, 31100, 23314,
+            32100, 23120, 41110,
+        ),
+        (
+            11300, 13300, 23304, 42110, 41100, 23320,
+        ),
+        (),
+        (
+            12310, 12300,
+        ),
+        (
+            31200, 11310, 21320, 32000, 41200, 42100, 30200, 22320, 33300, 43310,
+            32200, 33100, 41010, 30300, 43300, 43100,
+        ),
+        (
+            42200,
+        ),
+        (
+            32300, 43110, 42300, 33200, 31300, 43210, 42310, 41300, 40100, 40110,
+            43200, 42210, 41310, 40200, 33000, 40300, 43010,
+        ),
+        (
+            41210, 40310, 43000, 42010,
+        ),
+        (
+            42000, 41000, 40210,
         ),
         (),
         (),
         (
-            13110, 31100, 12300, 13300, 32100, 13100, 30200, 42100, 23120, 41110,
-            13310, 23320, 31200, 11310, 41200, 33200, 12310, 43200, 11300, 22320,
-            32200, 42200, 41210, 42210, 21320,
-        ),
-        (),
-        (
-            43210, 33300, 43310, 43300,
-        ),
-        (
-            33100, 43100, 43110,
-        ),
-        (
-            40200, 33000, 40210, 31300, 32300, 42300, 41300, 42310, 43000, 41310,
-            41100, 43010, 30300,
-        ),
-        (
-            40300, 42110,
-        ),
-        (
-            40310, 42000, 41000, 40100,
-        ),
-        (
-            42010, 40110,
-        ),
-        (),
-        (
             40000, 40010,
-        ),
-    ),
-    (
-        (
-            20004, 20013, 20001, 20011, 20014, 20003, 20012, 20002, 10100, 10210,
-            11000, 12010, 21002, 22011, 20103, 20214, 10110, 11010, 20101, 10200,
-            20111, 20113, 20102, 20112, 20202, 20204, 13000, 20212, 20211, 12000,
-            10300, 20201, 20304, 23003, 20120, 21020, 20220, 22020, 12100, 10310,
-            20020, 13010, 20314, 23013, 11100, 13100, 13200, 23020, 20320, 20301,
-            12110, 11110, 23204, 20311, 20302, 23103,
-        ),
-        (
-            22120, 20312, 13110, 21120, 23113, 23120, 13210, 23214,
-        ),
-        (),
-        (
-            12200, 11210, 12210, 32000, 11200, 13300, 21220, 22220, 23304, 23220,
-            30000, 42000,
-        ),
-        (
-            31000, 13310, 23314,
-        ),
-        (
-            23320, 11300,
-        ),
-        (
-            12300, 32100, 11310, 21320, 42100, 12310, 31100, 42110, 22320,
-        ),
-        (),
-        (
-            41110, 33200, 33300, 43300, 43310, 41100,
-        ),
-        (),
-        (
-            30100, 43200, 33100, 31200, 43100, 31300, 32300, 42300, 41300, 43110,
-            42310, 41310,
-        ),
-        (
-            41200, 43210, 33000, 32200, 42200, 40110, 30200, 42210, 30300, 43000,
-            40300, 40100, 41210, 40310,
-        ),
-        (
-            40200, 43010, 41000,
-        ),
-        (
-            40210, 42010, 41010,
-        ),
-        (
-            40000,
-        ),
-        (
-            40010,
         ),
     ),
 )
@@ -367,39 +366,37 @@
     return role, (CROSSED if kind == MID and way == INNER else SWAPPED)[near]
 
 
-def within_plane(kind, near):
-    return near == 0 or near == 3 or (near == 1 and kind == END)
-
-
 def parent(kind, role, near, part):
+    if kind == END and near == 1:
+        return INNER
     if role == ACROSS:
         return TO_X
     if role == ALONG:
         return TO_Y
-    if role == DIAGONAL and within_plane(kind, near):
+    if role == DIAGONAL and (near == 0 or near == 3):
         return (TO_Y, TO_X)[part]
-    if role == OWN and near == 0:
+    if near == 0:
         return None
     if near == 3:
         return FAR_END
-    return OUTER if kind == MID and near == 1 else INNER
+    return OUTER if near == 1 else INNER
 
 
 def children(kind, role, near, part):
-    if role == ACROSS:
-        return (ACROSS_Y,) if part == 0 and within_plane(kind, near) else ()
-    if role == ALONG:
-        return (ALONG_X,) if part == 1 and within_plane(kind, near) else ()
+    if kind == END and near == 1:
+        return ()
+    fed = kind == MID and (near == 0 or (near == 2 and role in (OWN, DIAGONAL)))
+    boxes = (OUTER_BOXES[role],) if fed else ()
+    if role == ACROSS or role == ALONG:
+        sided = (near == 0 or near == 3) and part == (0 if role == ACROSS else 1)
+        return boxes + ((ACROSS_Y if role == ACROSS else ALONG_X,) if sided else ())
     if role == DIAGONAL:
-        if near == 0:
-            return (DIAGONAL_INNER,)
-        return (DIAGONAL_OUTER,) if kind == MID and near == 2 else ()
-    boxes = (OWN_X, OWN_Y)
+        return boxes + ((DIAGONAL_INNER,) if near == 0 else ())
+    boxes += (OWN_X, OWN_Y)
     if near == 0:
         boxes += (OWN_INNER,)
-        boxes += (OWN_FAR_MID, OWN_FAR_END) if kind == END else (OWN_OUTER,)
-    if near == 2 and kind == MID:
-        boxes += (OWN_OUTER,)
+        if kind == END:
+            boxes += (OWN_FAR_MID, OWN_FAR_END)
     return boxes
 
 
@@ -427,6 +424,8 @@
     rows_ref,
     gu_ref,
     down_ref,
+    gu_turned_ref,
+    down_turned_ref,
     mixed_ref,
     hidden_ref,
     part_ref,
@@ -516,7 +515,7 @@
                 local.at[6 + 2 * owned + index],
             )
         )
-    for load in loads:
+    for load in loads[:6]:
         load.start()
     barrier = pltpu.get_barrier_semaphore()
     for kind, ways in ((END, (FAR_MID,)), (MID, (OUTER,))):
@@ -541,21 +540,31 @@
         + [jnp.zeros((lanes - experts, count), jnp.float32)],
         axis=0,
     )
-    rows_ref[mine, core, :, 2 * features :] = weights.T.astype(jnp.bfloat16)
+    weights = weights.T
+    side = weights[:half] + pltpu.roll(weights[half:], lanes // 2, 1)
+    rows_ref[mine, core, :half, 2 * features :] = side.astype(jnp.bfloat16)
     for load in loads[4:6]:
         load.wait()
     pl.semaphore_wait(barrier, 6)
+    for load in loads[6:]:
+        load.start()
 
     def piece(part):
         return pl.ds(part * half, half)
 
+    def span_of(part, width):
+        return pl.ds(0, width + lanes if part == 0 else width)
+
     def row_copy(role, near, part, way):
         at, to = place(role, near), place(*seen_from(kinds[0], way, role, near))
-        span = slice(None) if part is None else piece(part)
+        if part is None:
+            span = (slice(None), slice(None))
+        else:
+            span = (piece(part), span_of(part, 2 * features))
         index = 0 if part is None else part
         return pltpu.make_async_remote_copy(
-            src_ref=rows_ref.at[at, core, span],
-            dst_ref=rows_ref.at[to, core, span],
+            src_ref=rows_ref.at[(at, core) + span],
+            dst_ref=rows_ref.at[(to, core) + span],
             send_sem=sent.at[at, way * 2 + index],
             recv_sem=landed.at[to, core, index],
             device_id=targets_of[way],
@@ -574,10 +583,8 @@
             device_id_type=MESH,
         ).wait_recv()
 
-    def rows_by_columns(a, b):
-        return lax.dot_general(
-            a, b, (((1,), (1,)), ((), ())), preferred_element_type=jnp.float32
-        )
+    def rows_by_rows(a, b):
+        return jnp.dot(a, b, preferred_element_type=jnp.float32)
 
     def columns_by_columns(a, b):
         return lax.dot_general(
@@ -611,7 +618,13 @@
     def ahead(group):
         for role, near in GROUPS[group]:
             partner_rows(role, near)
-        side = stacked(rows_ref, group, 2 * features, lanes).astype(jnp.float32)
+        start, size = place(*GROUPS[group][0]), len(GROUPS[group])
+        packed = rows_ref[start : start + size, :, :half, 2 * features :].astype(jnp.float32)
+        packed = packed.reshape(2 * size * half, lanes)
+        turned = pltpu.roll(packed, lanes // 2, 1)
+        side = jnp.concatenate(
+            [packed.reshape(2 * size, half, lanes), turned.reshape(2 * size, half, lanes)], axis=1
+        ).reshape(2 * size * count, lanes)
         slots = lax.broadcasted_iota(jnp.int32, side.shape, 1)
         shape = (side.shape[0], hidden_units)
         units = lax.broadcasted_iota(jnp.int32, shape, 1)
@@ -623,8 +636,8 @@
         for index in range(owned):
             scale = jnp.sum(jnp.where(at_expert[index], side, 0.0), axis=1, keepdims=True)
             weight = jnp.where(of_expert[index], scale, weight)
-        mixed = rows_by_columns(stacked(rows_ref, group, 0, features), gu_ref[...])
-        raw_hidden = rows_by_columns(stacked(rows_ref, group, features, features), down_ref[...])
+        mixed = rows_by_rows(stacked(rows_ref, group, 0, features), gu_turned_ref[...])
+        raw_hidden = rows_by_rows(stacked(rows_ref, group, features, features), down_turned_ref[...])
         gate_pre = mixed[:, :hidden_units]
         up_part = mixed[:, hidden_units:]
         sigmoid_gate = jax.nn.sigmoid(gate_pre)
@@ -643,11 +656,16 @@
         ).astype(jnp.bfloat16)
         grad_up = (grad_hidden * active).astype(jnp.bfloat16)
         weighted = (hidden * weight).astype(jnp.bfloat16)
-        gate_side = gate_side.astype(jnp.bfloat16)
+        gate_side = gate_side.reshape(2 * size, count, lanes)
+        low = gate_side[:, :half].reshape(2 * size * half, lanes)
+        high = gate_side[:, half:].reshape(2 * size * half, lanes)
+        packed = (low + pltpu.roll(high, lanes // 2, 1)).astype(jnp.bfloat16)
+        part_ref[start : start + size, :, :half, features:] = packed.reshape(
+            size, 2, half, lanes
+        )
         keep(hidden_ref, group, 0, weighted)
         keep(mixed_ref, group, 0, grad_gate)
         keep(mixed_ref, group, hidden_units, grad_up)
-        keep(part_ref, group, features, gate_side)
 
     def back(group):
         dx = jnp.dot(
@@ -662,18 +680,22 @@
     def combine(role, near):
         at = place(role, near)
         pair_copy(at).wait_recv()
-        part_ref[at, core] = (
-            part_ref[at, core].astype(jnp.float32) + paired_ref[at].astype(jnp.float32)
-        ).astype(jnp.bfloat16)
+        for part in range(2):
+            span = (piece(part), span_of(part, features))
+            part_ref[(at, core) + span] = (
+                part_ref[(at, core) + span].astype(jnp.float32)
+                + paired_ref[(at,) + span].astype(jnp.float32)
+            ).astype(jnp.bfloat16)
 
     def box_index(box, near, part):
         return (box * depth + near) * 2 + part
 
     def sum_copy(role, near, part, way, box):
         index = box_index(box, seen_from(kinds[0], way, role, near)[1], part)
+        width = span_of(part, features)
         return pltpu.make_async_remote_copy(
-            src_ref=part_ref.at[place(role, near), core, piece(part)],
-            dst_ref=inbox_ref.at[index],
+            src_ref=part_ref.at[place(role, near), core, piece(part), width],
+            dst_ref=inbox_ref.at[index, :, width],
             send_sem=sums_sent.at[box_index(box, near, part)],
             recv_sem=sums_landed.at[index],
             device_id=targets_of[way],
@@ -682,15 +704,16 @@
 
     def incoming(role, near, part, box):
         index = box_index(box, near, part)
+        width = span_of(part, features)
         pltpu.make_async_remote_copy(
-            src_ref=inbox_ref.at[index],
-            dst_ref=inbox_ref.at[index],
+            src_ref=inbox_ref.at[index, :, width],
+            dst_ref=inbox_ref.at[index, :, width],
             send_sem=sums_sent.at[index],
             recv_sem=sums_landed.at[index],
             device_id=targets_of[PARTNER],
             device_id_type=MESH,
         ).wait_recv()
-        return inbox_ref[index].astype(jnp.float32)
+        return inbox_ref[index, :, width].astype(jnp.float32)
 
     def home_box(role, way):
         if way == TO_X:
@@ -700,7 +723,7 @@
         if way == FAR_END:
             return OWN_FAR_END if kinds[0] == END else OWN_FAR_MID
         if kinds[0] == END:
-            return OWN_OUTER if role == OWN else DIAGONAL_OUTER
+            return OUTER_BOXES[role]
         return OWN_INNER if role == OWN else DIAGONAL_INNER
 
     def gather_sums(role, near, part):
@@ -708,14 +731,16 @@
         at = place(role, near)
         boxes, way = children(kind, role, near, part), parent(kind, role, near, part)
         if boxes:
-            value = part_ref[at, core, piece(part)].astype(jnp.float32)
+            span = (piece(part), span_of(part, features))
+            value = part_ref[(at, core) + span].astype(jnp.float32)
             for box in boxes:
                 value = value + incoming(role, near, part, box)
             if way is None:
                 tokens_out[piece(part), :] = value[:, :features].astype(jnp.bfloat16)
-                gate_sums_ref[piece(part), :] = value[:, features:]
+                if part == 0:
+                    gate_sums_ref[...] = value[:, features:]
             else:
-                part_ref[at, core, piece(part)] = value.astype(jnp.bfloat16)
+                part_ref[(at, core) + span] = value.astype(jnp.bfloat16)
         if way is not None:
             begin(sum_copy, role, near, part, way, home_box(role, way))
 
@@ -761,16 +786,26 @@
         stages.append((ahead, (group,)))
         stages.append((back, (group,)))
     stages += [(weight_grad, job) for job in jobs]
+    def opening(codes):
+        return next(index for index, code in enumerate(codes) if code // 10000 == ARRIVE)
+
+    for kind in (END, MID):
+        codes = SCHEDULE[kind][0]
+        within(kind, functools.partial(play, codes[: opening(codes)]))
+    for load in loads[6:]:
+        load.wait()
+    for ref, turned_ref in ((gu_ref, gu_turned_ref), (down_ref, down_turned_ref)):
+        for first in range(0, features, 512):
+            turned_ref[first : first + 512, :] = ref[:, first : first + 512].T
     for index, codes in enumerate(zip(*SCHEDULE, strict=True)):
         for kind in (END, MID):
-            if codes[kind]:
-                within(kind, functools.partial(play, codes[kind]))
-        if index == 0:
-            for load in loads[6:]:
-                load.wait()
+            steps = codes[kind][opening(codes[kind]) :] if index == 0 else codes[kind]
+            if steps:
+                within(kind, functools.partial(play, steps))
         if index < len(stages):
             stages[index][0](*stages[index][1])
-    sums = gate_sums_ref[...].T
+    packed = gate_sums_ref[...]
+    sums = jnp.concatenate([packed, pltpu.roll(packed, lanes // 2, 1)], axis=0).T
     picked = jnp.zeros(routing.shape, jnp.float32)
     for index in range(experts):
         picked = jnp.where(routing == index, sums[index : index + 1], picked)
@@ -804,7 +839,7 @@
     experts = owned * size
     depth = size // 2
     chips = 4 * depth
-    lanes = (experts + 127) // 128 * 128
+    lanes = (2 * experts + 127) // 128 * 128
     kind = jnp.bfloat16
     width, sums = 2 * features + lanes, features + lanes
     outside = pl.BlockSpec(memory_space=pltpu.HBM)
@@ -827,12 +862,14 @@
             pltpu.VMEM((chips, 2, count, width), kind),
             pltpu.VMEM((2 * units, features), kind),
             pltpu.VMEM((units, features), kind),
+            pltpu.VMEM((features, 2 * units), kind),
+            pltpu.VMEM((features, units), kind),
             pltpu.VMEM((chips, 2 * count, 2 * units), kind),
             pltpu.VMEM((chips, 2 * count, units), kind),
             pltpu.VMEM((chips, 2, count, sums), kind),
             pltpu.VMEM((chips, count, sums), kind),
             pltpu.VMEM((boxes, count // 2, sums), kind),
-            pltpu.VMEM((count, lanes), jnp.float32),
+            pltpu.VMEM((count // 2, lanes), jnp.float32),
             pltpu.VMEM(turned, jnp.int32),
             pltpu.VMEM(turned, jnp.int32),
             pltpu.VMEM(turned, kind),

time: 64.7 us -> 62.7 us (0.969)
  Pallas kernels: 63.7 us -> 61.7 us
    pallas_call x1, Pallas kernels: 61.5 us -> 59.4 us  [fused_layer(): pl.pallas_call(functools.partial(fused_kernel, experts), out_shape=tuple(...]
where the time goes in v3:
time: 62.7 us; the launch traced here: 62.5 us
  Pallas kernels  61.7 us (98%)
  between operations  0.8 us (1%)
    pallas_call x1, Pallas kernels, fused_layer(): pl.pallas_call(functools.partial(fused_kernel, experts), out_shape=tuple(...  59.4 us
    pallas_call x1, Pallas kernels, fused_layer(): pl.pallas_call(finish_kernel, out_shape=tuple((jax.ShapeDtypeStruct(*resu...  2.26 us

profile of v3, /device:TPU:0, one launch (start us, length us, event | category | flops | bytes accessed | tf_op | source)
XLA Modules:
  0.0 62.5 jit_solution(7630577268696454501)
XLA Ops:
  0.6 59.4 %shard_map.111 = (bf16[32,2048]{1,0:T(8,128)(2,1)S(1)}, f32[8,32]{1,0:T(8,128)S(1)}, bf16[2,2,192,2048]{3,2,1,0:T(8,128)(2,1)S(1)}, bf16[2,192,2048]{2,1,0:T(8,128)(2,1)S(1)}) custom-call(bf16[32,2048]{1,0:T(8,128)(2,1)} %tokens_hbm.1, bf16[32,2048]{1,0:T(8,128)(2,1)} %grad_out_hbm.1, s32[8,32]{1,0:T(8,128)} %bitcast.4, s32[8,32]{1,0:T(8,128)} %bitcast.5, ...), custom_call_target="tpu_custom_call" | custom-call | tf_op jit(solution)/shard_map/pallas_call | solution.py:856
  60.1 2.3 %shard_map.112 = (bf16[32,2048]{1,0:T(8,128)(2,1)}, f32[8,32]{1,0:T(8,128)}, bf16[2,2,192,2048]{3,2,1,0:T(8,128)(2,1)}, bf16[2,192,2048]{2,1,0:T(8,128)(2,1)}) custom-call(bf16[32,2048]{1,0:T(8,128)(2,1)S(1)} %get-tuple-element.12.refs_0_, f32[8,32]{1,0:T(8,128)S(1)} %get-tuple-element.13.refs_1_, bf16[2,2,192,2048]{3,2,1,0:T(8,128)(2,1)S(1)} %get-tuple-element.14.refs_2_, ...), custom_call_target="tpu_custom_call" | custom-call | tf_op jit(solution)/shard_map/pallas_call | solution.py:896

commit v4 on v3

--- a/solution.py
+++ b/solution.py
@@ -518,14 +518,12 @@
     for load in loads[:6]:
         load.start()
     barrier = pltpu.get_barrier_semaphore()
-    for kind, ways in ((END, (FAR_MID,)), (MID, (OUTER,))):
-
-        @pl.when(is_end if kind == END else is_mid)
-        def _():
-            for way in (PARTNER, TO_X, TO_Y, INNER, FAR_END) + ways:
-                pl.semaphore_signal(
-                    barrier, inc=1, device_id=targets_of[way], device_id_type=MESH
-                )
+    for way in (PARTNER, TO_X, TO_Y, INNER):
+        pl.semaphore_signal(barrier, inc=1, device_id=targets_of[way], device_id_type=MESH)
+
+    @pl.when(is_mid)
+    def _():
+        pl.semaphore_signal(barrier, inc=1, device_id=targets_of[OUTER], device_id_type=MESH)
 
     for load in loads[:4]:
         load.wait()
@@ -545,7 +543,7 @@
     rows_ref[mine, core, :half, 2 * features :] = side.astype(jnp.bfloat16)
     for load in loads[4:6]:
         load.wait()
-    pl.semaphore_wait(barrier, 6)
+    pl.semaphore_wait(barrier, 4 + is_mid.astype(jnp.int32))
     for load in loads[6:]:
         load.start()
 

time: 62.7 us -> 61.7 us (0.984)
  Pallas kernels: 61.7 us -> 60.8 us
    pallas_call x1, Pallas kernels: 59.4 us -> 58.5 us  [fused_layer(): pl.pallas_call(functools.partial(fused_kernel, experts), out_shape=tuple(...]
where the time goes in v4:
time: 61.7 us; the launch traced here: 61.6 us
  Pallas kernels  60.8 us (99%)
  between operations  0.8 us (1%)
    pallas_call x1, Pallas kernels, fused_layer(): pl.pallas_call(functools.partial(fused_kernel, experts), out_shape=tuple(...  58.5 us
    pallas_call x1, Pallas kernels, fused_layer(): pl.pallas_call(finish_kernel, out_shape=tuple((jax.ShapeDtypeStruct(*resu...  2.26 us

profile of v4, /device:TPU:0, one launch (start us, length us, event | category | flops | bytes accessed | tf_op | source)
XLA Modules:
  0.0 61.6 jit_solution(5915659803382865183)
XLA Ops:
  0.6 58.5 %shard_map.111 = (bf16[32,2048]{1,0:T(8,128)(2,1)S(1)}, f32[8,32]{1,0:T(8,128)S(1)}, bf16[2,2,192,2048]{3,2,1,0:T(8,128)(2,1)S(1)}, bf16[2,192,2048]{2,1,0:T(8,128)(2,1)S(1)}) custom-call(bf16[32,2048]{1,0:T(8,128)(2,1)} %tokens_hbm.1, bf16[32,2048]{1,0:T(8,128)(2,1)} %grad_out_hbm.1, s32[8,32]{1,0:T(8,128)} %bitcast.4, s32[8,32]{1,0:T(8,128)} %bitcast.5, ...), custom_call_target="tpu_custom_call" | custom-call | tf_op jit(solution)/shard_map/pallas_call | solution.py:854
  59.1 2.3 %shard_map.112 = (bf16[32,2048]{1,0:T(8,128)(2,1)}, f32[8,32]{1,0:T(8,128)}, bf16[2,2,192,2048]{3,2,1,0:T(8,128)(2,1)}, bf16[2,192,2048]{2,1,0:T(8,128)(2,1)}) custom-call(bf16[32,2048]{1,0:T(8,128)(2,1)S(1)} %get-tuple-element.12.refs_0_, f32[8,32]{1,0:T(8,128)S(1)} %get-tuple-element.13.refs_1_, bf16[2,2,192,2048]{3,2,1,0:T(8,128)(2,1)S(1)} %get-tuple-element.14.refs_2_, ...), custom_call_target="tpu_custom_call" | custom-call | tf_op jit(solution)/shard_map/pallas_call | solution.py:894
